TPU v7x, 32 devices: a whole 2x2x4 slice. The times are simulated.
32 devices in a mesh: group: 2 (over y), wide: 8 (over z, x), narrow: 2 (over core).
Axes of the slice: x: 2, y: 2, z: 4, core: 2. Of those that a mesh axis runs over, the one named last changes fastest.
Arguments:
- hidden_in: bfloat16 [16, 16384], P(('group', 'wide'), 'narrow'), parts along dimension 0, may hold values from -60 to 60
- norm_gain: float32 [16384], P('narrow'), may hold values from 0.1 to 1.9
- qkv_weight: bfloat16 [16384, 9216], P('narrow', 'wide'), may hold values from -0.046875 to 0.046875
- out_weight: bfloat16 [8192, 16384], P('narrow', 'wide'), may hold values from -0.25 to 0.25
- cache_keys: bfloat16 [16, 256, 512], P(('group', 'wide'), None, 'narrow'), parts along dimension 0, may hold values from -500 to 500
- cache_values: bfloat16 [16, 256, 512], P(('group', 'wide'), None, 'narrow'), parts along dimension 0, may hold values from -6 to 6
- cache_lengths: int32 [16], P(('group', 'wide')), parts along dimension 0, may hold values from 4 to 256, as said below
Outputs:
- layer_out: float32 [16, 16384], P(('group', 'wide'), 'narrow'), parts along dimension 0
There are 2 independent parts, one for each index of `group`. A program takes and returns all parts, laid end to end along the dimension named above; an argument that names none is the same for every part. Nothing has to cross between parts.
Inputs may be any that keep to these rules, and one draw needn't show every extreme that they name: Some row's length is exactly 256 in every draw; row r's cached positions are 0 to cache_lengths[r] - 1 and its new token stands at position cache_lengths[r].
All inputs are finite; a program needn't handle non-finite values.
Results may differ from a plain program's by a relative error of at most 0.0058.
Values may be sent and summed in bfloat16 or wider, within the bound.
No kernel may reach another device: no remote copies, remote signals or barrier semaphores. Data moves between devices by JAX's collectives and lax.ppermute only.
A program may use at most 64 MiB of HBM per device.

v0:
```python
import functools

import jax
import jax.numpy as jnp
from jax import lax
from jax.experimental import pallas as pl
from jax.experimental.pallas import tpu as pltpu
from jax.sharding import PartitionSpec as P

D = 16384
HD = 128
LANES = 128

rope_theta = 500000.0
norm_eps = 1e-05

VMEM = pl.BlockSpec(memory_space=pltpu.VMEM)
SMEM = pl.BlockSpec(memory_space=pltpu.SMEM)
HBM = pl.BlockSpec(memory_space=pl.ANY)


def params(limit):
    return pltpu.CompilerParams(vmem_limit_bytes=limit)


def cost(flops, size):
    return pl.CostEstimate(flops=flops, bytes_accessed=size, transcendentals=0)


def rope_tables(lengths):
    half = HD // 2
    frequency = rope_theta ** (-jnp.arange(half, dtype=jnp.float32) * 2.0 / HD)
    angles = lengths.astype(jnp.float32) * frequency
    cosine = jnp.cos(angles)
    sine = jnp.sin(angles)
    return jnp.stack([jnp.concatenate([cosine, cosine]), jnp.concatenate([-sine, sine])])


def square_kernel(x_ref, f_ref, s_ref):
    tiles = f_ref.shape[0]
    for j in range(tiles):
        f_ref[j : j + 1, :] = x_ref[:, j * LANES : (j + 1) * LANES].astype(jnp.float32)
    values = f_ref[...]
    s_ref[...] = jnp.sum((values * values).reshape(-1, 8, LANES), axis=0)


def norm_kernel(f_ref, g_ref, own_ref, other_ref, o_ref):
    total = jnp.sum(own_ref[...] + other_ref[...], keepdims=True)
    scale = lax.rsqrt(total / D + norm_eps)
    normed = (f_ref[...] * scale * g_ref[...]).astype(jnp.bfloat16)
    for j in range(o_ref.shape[0]):
        o_ref[j] = normed


def product_kernel(x_ref, w_ref, o_ref):
    result = jnp.dot(x_ref[...], w_ref[...], preferred_element_type=jnp.float32)
    for r in range(result.shape[0]):
        o_ref[r] = result[r : r + 1, :]


def product(x, w):
    rows, depth = x.shape
    cols = w.shape[1]
    return pl.pallas_call(
        product_kernel,
        out_shape=jax.ShapeDtypeStruct((rows, 1, cols), jnp.float32),
        in_specs=[VMEM, VMEM],
        out_specs=VMEM,
        compiler_params=params(4 << 20),
        cost_estimate=cost(2 * rows * depth * cols, w.size * 2),
    )(x, w)


def turn(values, table):
    half = values.shape[-1] // 2
    swapped = pltpu.roll(values, half, 1)
    return values * table[0:1, :] + swapped * table[1:2, :]


def attend_kernel(joined_ref, length, table, k_ref, v_ref, o_ref):
    groups, slots, head_dim = joined_ref.shape
    share = slots - 2
    capacity = k_ref.shape[0]
    live = lax.broadcasted_iota(jnp.int32, (share, capacity), 1) < length
    for g in range(groups):
        lanes = slice(g * head_dim, (g + 1) * head_dim)
        query = (turn(joined_ref[g, :share, :], table) * head_dim ** (-0.5)).astype(jnp.bfloat16)
        new_key = turn(joined_ref[g, share : share + 1, :], table).astype(jnp.bfloat16)
        new_value = joined_ref[g, share + 1 : share + 2, :].astype(jnp.bfloat16).astype(jnp.float32)
        scores = lax.dot_general(
            query, k_ref[:, lanes], (((1,), (1,)), ((), ())), preferred_element_type=jnp.float32
        )
        own = jnp.sum(query.astype(jnp.float32) * new_key.astype(jnp.float32), -1, keepdims=True)
        scores = jnp.where(live, scores, -1e30)
        top = jnp.maximum(jnp.max(scores, -1, keepdims=True), own)
        expo = jnp.exp(scores - top)
        own_expo = jnp.exp(own - top)
        total = jnp.sum(expo, -1, keepdims=True) + own_expo
        probs = (expo / total).astype(jnp.bfloat16)
        mixed = jnp.dot(probs, v_ref[:, lanes], preferred_element_type=jnp.float32)
        mixed = (mixed + (own_expo / total) * new_value).astype(jnp.bfloat16)
        for j in range(o_ref.shape[0]):
            o_ref[j, g * share : (g + 1) * share, :] = mixed


def direct_kernel(core_ref, len_ref, own_ref, other_ref, table_ref, k_ref, v_ref, o_ref, joined):
    half = own_ref.shape[0] // 2
    cols = own_ref.shape[2]
    groups, slots, _ = joined.shape
    first = core_ref[0] * half
    for b in range(half):
        for c in range(cols // LANES):
            piece = b * (cols // LANES) + c
            lanes = slice(c * LANES, (c + 1) * LANES)
            joined[piece // slots, piece % slots : piece % slots + 1, :] = (
                own_ref[first + b, :, lanes] + other_ref[first + b, :, lanes]
            )
    attend_kernel(joined, len_ref[0], table_ref[...], k_ref, v_ref, o_ref)


def given_kernel(len_ref, joined_ref, table_ref, k_ref, v_ref, o_ref):
    attend_kernel(joined_ref, len_ref[0], table_ref[...], k_ref, v_ref, o_ref)


def add_kernel(core_ref, x_ref, own_ref, other_ref, o_ref):
    half = own_ref.shape[0] // 2
    cols = own_ref.shape[2]
    first = core_ref[0] * half
    for b in range(half):
        lanes = slice(b * cols, (b + 1) * cols)
        added = own_ref[first + b] + other_ref[first + b]
        o_ref[:, lanes] = x_ref[:, lanes].astype(jnp.float32) + added


def swap(x):
    return lax.ppermute(x, "narrow", [(0, 1), (1, 0)])


def exchange(x):
    return lax.all_to_all(x, "wide", split_axis=0, concat_axis=0, tiled=True)


def body(hidden_in, norm_gain, qkv_weight, out_weight, cache_keys, cache_values, cache_lengths):
    wide = lax.axis_size("wide")
    core = lax.axis_index("narrow").astype(jnp.int32).reshape(1)
    table = rope_tables(cache_lengths)
    lengths = cache_lengths
    hidden_in, core, table, lengths = lax.optimization_barrier((hidden_in, core, table, lengths))
    feats = hidden_in.shape[1]
    tiles = feats // LANES
    values, squares = pl.pallas_call(
        square_kernel,
        out_shape=(
            jax.ShapeDtypeStruct((tiles, LANES), jnp.float32),
            jax.ShapeDtypeStruct((8, LANES), jnp.float32),
        ),
        in_specs=[VMEM],
        out_specs=(VMEM, VMEM),
        compiler_params=params(4 << 20),
        cost_estimate=cost(1000, 64_000),
    )(hidden_in)
    normed = pl.pallas_call(
        norm_kernel,
        out_shape=jax.ShapeDtypeStruct((wide, tiles, LANES), jnp.bfloat16),
        in_specs=[VMEM] * 4,
        out_specs=VMEM,
        compiler_params=params(4 << 20),
        cost_estimate=cost(1000, 40_000_000),
    )(values, norm_gain.reshape(tiles, LANES), squares, swap(squares))
    gathered = exchange(normed)
    partial_qkv = product(gathered.reshape(wide, feats), qkv_weight)
    moved = exchange(partial_qkv)
    other = swap(moved)
    capacity = cache_keys.shape[1]
    groups = cache_keys.shape[2] // HD
    keys = cache_keys.reshape(capacity, groups * HD)
    cached = cache_values.reshape(capacity, groups * HD)
    block = moved.shape[2]
    slots = wide // 2 * block // (groups * HD)
    share = slots - 2
    depth = groups * share * HD
    mixed_shape = jax.ShapeDtypeStruct((wide, depth // LANES, LANES), jnp.bfloat16)
    if block % LANES == 0:
        mixed = pl.pallas_call(
            direct_kernel,
            out_shape=mixed_shape,
            in_specs=[SMEM, SMEM, VMEM, VMEM, VMEM, VMEM, VMEM],
            out_specs=VMEM,
            scratch_shapes=[pltpu.VMEM((groups, slots, HD), jnp.float32)],
            compiler_params=params(4 << 20),
            cost_estimate=cost(1000, 40_000_000),
        )(core, lengths, moved, other, table, keys, cached)
    else:
        first = core[0] * (wide // 2)
        joined = lax.dynamic_slice_in_dim(moved + other, first, wide // 2, 0)
        mixed = pl.pallas_call(
            given_kernel,
            out_shape=mixed_shape,
            in_specs=[SMEM, VMEM, VMEM, VMEM, VMEM],
            out_specs=VMEM,
            compiler_params=params(4 << 20),
            cost_estimate=cost(1000, 40_000_000),
        )(lengths, joined.reshape(groups, slots, HD), table, keys, cached)
    spread = exchange(mixed)
    partial_out = product(spread.reshape(wide, depth), out_weight)
    added = exchange(partial_out)
    return pl.pallas_call(
        add_kernel,
        out_shape=jax.ShapeDtypeStruct((1, feats), jnp.float32),
        in_specs=[SMEM, VMEM, VMEM, VMEM],
        out_specs=VMEM,
        compiler_params=params(4 << 20),
        cost_estimate=cost(1000, 1_000_000),
    )(core, hidden_in, added, swap(added))


def solution(mesh):
    placed = (
        P(("group", "wide"), "narrow"),
        P("narrow"),
        P("narrow", "wide"),
        P("narrow", "wide"),
        P(("group", "wide"), None, "narrow"),
        P(("group", "wide"), None, "narrow"),
        P(("group", "wide")),
    )
    return jax.shard_map(
        body, mesh=mesh, in_specs=placed, out_specs=P(("group", "wide"), "narrow"), check_vma=False
    )
```

profile of v0, /device:TPU:0, one launch (start us, length us, event | category | flops | bytes accessed | tf_op | source)
XLA Modules:
  0.0 61.6 jit_solution(14920947227994730035)
XLA Ops:
  0.0 0.0 copy-start.3
  0.0 0.0 copy-start.2
  0.7 0.1 fusion.2
  0.8 0.1 fusion
  0.8 0.1 maximum_bitcast_fusion
  0.9 0.1 maximum_bitcast_fusion.1
  1.0 0.0 copy-start.4
  1.0 0.8 %copy-done.4 = bf16[1,8192]{1,0:T(2,128)(2,1)S(1)} copy-done((bf16[1,8192]{1,0:T(2,128)(2,1)S(1)}, bf16[1,8192]{1,0:T(2,128)(2,1)}, u32[]{:S(2)}) %copy-start.4) | copy-done | bytes 16408
  1.7 0.0 copy-start.5
  1.8 0.6 collective-permute-start
  2.3 0.8 %collective-permute-done.other_ref = f32[8,128]{1,0:T(8,128)S(1)} collective-permute-done((f32[8,128]{1,0:T(8,128)S(1)}, f32[8,128]{1,0:T(8,128)S(1)}, u32[]{:S(2)}, u32[]{:S(2)}) %collective-permute-start) | collective-permute-done | bytes 4128 | tf_op jit(solution)/shard_map/ppermute | solution.py:136
  3.2 0.0 copy-start.6
  3.2 0.8 %copy-done.6 = f32[8192]{0:T(1024)S(1)} copy-done((f32[8192]{0:T(1024)S(1)}, f32[8192]{0:T(1024)}, u32[]{:S(2)}) %copy-start.6) | copy-done | bytes 32792
  3.9 0.1 shard_map.74
  4.1 14.3 %all_to_all.20 = bf16[8,64,128]{2,1,0:T(8,128)(2,1)S(1)} all-to-all(bf16[8,64,128]{2,1,0:T(8,128)(2,1)S(1)} %shard_map.74), channel_id=1, replica_groups=mesh['group'=2,'wide'=8,'narrow'=2] {'wide'}, dimensions={0} | all-to-all | bytes 262144 | tf_op jit(solution)/shard_map/all_to_all | solution.py:140
  18.3 0.1 copy.12
  18.4 0.0 copy-start
  18.4 6.4 %copy-done = bf16[8192,1152]{1,0:T(8,128)(2,1)S(1)} copy-done((bf16[8192,1152]{1,0:T(8,128)(2,1)S(1)}, bf16[8192,1152]{1,0:T(8,128)(2,1)}, u32[]{:S(2)}) %copy-start) | copy-done | bytes 18874392
  24.8 0.0 copy-start.1
  24.8 2.5 %shard_map.75 = f32[8,1,1152]{2,1,0:T(1,128)S(1)} custom-call(bf16[8,8192]{1,0:T(8,128)(2,1)S(1)} %bitcast.17, bf16[8192,1152]{1,0:T(8,128)(2,1)S(1)} %copy-done), custom_call_target="tpu_custom_call" | custom-call | flops 150994944 | bytes 18874368 | tf_op jit(solution)/shard_map/pallas_call | solution.py:64
  27.3 9.5 %all_to_all.21.own_ref = f32[8,1,1152]{2,1,0:T(1,128)S(1)} all-to-all(f32[8,1,1152]{2,1,0:T(1,128)S(1)} %shard_map.75), channel_id=1, replica_groups=mesh['group'=2,'wide'=8,'narrow'=2] {'wide'}, dimensions={0} | all-to-all | bytes 73728 | tf_op jit(solution)/shard_map/all_to_all | solution.py:140
  36.8 0.0 collective-permute-start.1
  36.8 1.2 %collective-permute-done.1.other_ref = f32[8,1,1152]{2,1,0:T(1,128)S(1)} collective-permute-done((f32[8,1,1152]{2,1,0:T(1,128)S(1)}, f32[8,1,1152]{2,1,0:T(1,128)S(1)}, u32[]{:S(2)}, u32[]{:S(2)}) %collective-permute-start.1) | collective-permute-done | bytes 36896 | tf_op jit(solution)/shard_map/ppermute | solution.py:136
  38.0 0.0 copy-done.3
  38.0 0.0 copy-done.2
  38.0 0.8 %shard_map.76 = bf16[8,32,128]{2,1,0:T(8,128)(2,1)S(1)} custom-call(s32[1]{0:T(128)} %bitcast.core_ref, s32[1]{0:T(128)S(6)} %copy.14.len_ref, f32[8,1,1152]{2,1,0:T(1,128)S(1)} %all_to_all.21.own_ref, f32[8,1,1152]{2,1,0:T(1,128)S(1)} %collective-permute-done.1.other_ref, f32[2,128]{1,0:T(2,128)S(1)} %pad_maximum_fusion.table_ref, ...), custom_call_target="tpu_custom_call" | custom-call | flops 1000 | bytes 40000000 | tf_op jit(solution)/shard_map/pallas_call | solution.py:184
  38.9 9.3 %all_to_all.22 = bf16[8,32,128]{2,1,0:T(8,128)(2,1)S(1)} all-to-all(bf16[8,32,128]{2,1,0:T(8,128)(2,1)S(1)} %shard_map.76), channel_id=1, replica_groups=mesh['group'=2,'wide'=8,'narrow'=2] {'wide'}, dimensions={0} | all-to-all | bytes 131072 | tf_op jit(solution)/shard_map/all_to_all | solution.py:140
  48.2 0.0 copy-done.1
  48.2 2.3 %shard_map.77 = f32[8,1,2048]{2,1,0:T(1,128)S(1)} custom-call(bf16[8,4096]{1,0:T(8,128)(2,1)S(1)} %bitcast.18, bf16[4096,2048]{1,0:T(8,128)(2,1)S(1)} %copy-done.1), custom_call_target="tpu_custom_call" | custom-call | flops 134217728 | bytes 16777216 | tf_op jit(solution)/shard_map/pallas_call | solution.py:64
  50.5 9.3 %all_to_all.23.own_ref = f32[8,1,2048]{2,1,0:T(1,128)S(1)} all-to-all(f32[8,1,2048]{2,1,0:T(1,128)S(1)} %shard_map.77), channel_id=1, replica_groups=mesh['group'=2,'wide'=8,'narrow'=2] {'wide'}, dimensions={0} | all-to-all | bytes 131072 | tf_op jit(solution)/shard_map/all_to_all | solution.py:140
  59.7 0.0 collective-permute-start.2
  59.7 1.3 %collective-permute-done.2.other_ref = f32[8,1,2048]{2,1,0:T(1,128)S(1)} collective-permute-done((f32[8,1,2048]{2,1,0:T(1,128)S(1)}, f32[8,1,2048]{2,1,0:T(1,128)S(1)}, u32[]{:S(2)}, u32[]{:S(2)}) %collective-permute-start.2) | collective-permute-done | bytes 65568 | tf_op jit(solution)/shard_map/ppermute | solution.py:136
  61.0 0.0 copy-done.5
  61.0 0.6 %shard_map.78 = f32[1,8192]{1,0:T(1,128)} custom-call(s32[1]{0:T(128)} %bitcast.core_ref, bf16[1,8192]{1,0:T(2,128)(2,1)S(1)} %copy-done.5, f32[8,1,2048]{2,1,0:T(1,128)S(1)} %all_to_all.23.own_ref, f32[8,1,2048]{2,1,0:T(1,128)S(1)} %collective-permute-done.2.other_ref), custom_call_target="tpu_custom_call" | custom-call | flops 1000 | bytes 1000000 | tf_op jit(solution)/shard_map/pallas_call | solution.py:207
  (3 shorter events, 0.1 us)
Async XLA Ops:
  0.0 38.0 %copy-start.3 = (bf16[1,256,256]{2,1,0:T(8,128)(2,1)S(1)}, bf16[1,256,256]{2,1,0:T(8,128)(2,1)}, u32[]{:S(2)}) copy-start(bf16[1,256,256]{2,1,0:T(8,128)(2,1)} %param.12) | copy-start | bytes 393220
  0.0 38.0 %copy-start.2 = (bf16[1,256,256]{2,1,0:T(8,128)(2,1)S(1)}, bf16[1,256,256]{2,1,0:T(8,128)(2,1)}, u32[]{:S(2)}) copy-start(bf16[1,256,256]{2,1,0:T(8,128)(2,1)} %param.11) | copy-start | bytes 393220
  1.0 0.8 %copy-start.4 = (bf16[1,8192]{1,0:T(2,128)(2,1)S(1)}, bf16[1,8192]{1,0:T(2,128)(2,1)}, u32[]{:S(2)}) copy-start(bf16[1,8192]{1,0:T(2,128)(2,1)} %x_ref.1) | copy-start | bytes 49156
  1.7 59.3 %copy-start.5 = (bf16[1,8192]{1,0:T(2,128)(2,1)S(1)}, bf16[1,8192]{1,0:T(2,128)(2,1)}, u32[]{:S(2)}) copy-start(bf16[1,8192]{1,0:T(2,128)(2,1)} %x_ref.1) | copy-start | bytes 49156
  1.8 1.4 %collective-permute-start = (f32[8,128]{1,0:T(8,128)S(1)}, f32[8,128]{1,0:T(8,128)S(1)}, u32[]{:S(2)}, u32[]{:S(2)}) collective-permute-start(f32[8,128]{1,0:T(8,128)S(1)} %get-tuple-element.15.own_ref), channel_id=1, source_target_pairs={{0,1},{1,0},{2,3},{3,2},{4,5},{5,4},{6,7},{7,6},{8,9},{9,8},{10,11... | collective-permute-start | bytes 12296 | tf_op jit(solution)/shard_map/ppermute | solution.py:136
  3.2 0.8 %copy-start.6 = (f32[8192]{0:T(1024)S(1)}, f32[8192]{0:T(1024)}, u32[]{:S(2)}) copy-start(f32[8192]{0:T(1024)} %param.8) | copy-start | bytes 98308
  18.4 6.4 %copy-start = (bf16[8192,1152]{1,0:T(8,128)(2,1)S(1)}, bf16[8192,1152]{1,0:T(8,128)(2,1)}, u32[]{:S(2)}) copy-start(bf16[8192,1152]{1,0:T(8,128)(2,1)} %w_ref.2) | copy-start | bytes 56623108
  24.8 23.4 %copy-start.1 = (bf16[4096,2048]{1,0:T(8,128)(2,1)S(1)}, bf16[4096,2048]{1,0:T(8,128)(2,1)}, u32[]{:S(2)}) copy-start(bf16[4096,2048]{1,0:T(8,128)(2,1)} %w_ref.3) | copy-start | bytes 50331652
  36.8 1.2 %collective-permute-start.1 = (f32[8,1,1152]{2,1,0:T(1,128)S(1)}, f32[8,1,1152]{2,1,0:T(1,128)S(1)}, u32[]{:S(2)}, u32[]{:S(2)}) collective-permute-start(f32[8,1,1152]{2,1,0:T(1,128)S(1)} %all_to_all.21.own_ref), channel_id=1, source_target_pairs={{0,1},{1,0},{2,3},{3,2},{4,5},{5,4},{6,7},{7,6},{8,9},{9,8},{10,11... | collective-permute-start | bytes 110600 | tf_op jit(solution)/shard_map/ppermute | solution.py:136
  59.7 1.3 %collective-permute-start.2 = (f32[8,1,2048]{2,1,0:T(1,128)S(1)}, f32[8,1,2048]{2,1,0:T(1,128)S(1)}, u32[]{:S(2)}, u32[]{:S(2)}) collective-permute-start(f32[8,1,2048]{2,1,0:T(1,128)S(1)} %all_to_all.23.own_ref), channel_id=1, source_target_pairs={{0,1},{1,0},{2,3},{3,2},{4,5},{5,4},{6,7},{7,6},{8,9},{9,8},{10,11... | collective-permute-start | bytes 196616 | tf_op jit(solution)/shard_map/ppermute | solution.py:136
where the time goes:
time: 62 us; the launch traced here: 61.6 us
  blocking collectives  42.3 us (68%)
  local copies, waits for them, and re-layouts  8.01 us (13%)
  Pallas kernels  6.42 us (10%)
  waiting for transfers between devices  3.29 us (5%)
  between operations  0.76 us (1%)
    all_to_all x4, blocking collectives, exchange(): return lax.all_to_all(x, 'wide', split_axis=0, concat_axis=0, tiled=True)  42.3 us
    unnamed x16, local copies, waits for them, and re-layouts  8.01 us
    pallas_call x2, Pallas kernels, product(): pl.pallas_call(product_kernel, out_shape=jax.ShapeDtypeStruct((rows, 1, c...  4.82 us
    ppermute x3, waiting for transfers between devices, swap(): return lax.ppermute(x, 'narrow', [(0, 1), (1, 0)])  3.29 us
  transfers between devices with their start and end apart: 3, of which 3 were waited for; matrix products, arithmetic and copies ran while one was open for 0% of the time, Pallas kernels for 0%

commit v1 on v0

--- a/solution.py
+++ b/solution.py
@@ -165,7 +165,7 @@
         in_specs=[VMEM] * 4,
         out_specs=VMEM,
         compiler_params=params(4 << 20),
-        cost_estimate=cost(1000, 40_000_000),
+        cost_estimate=cost(40_000_000_000, 40_000_000),
     )(values, norm_gain.reshape(tiles, LANES), squares, swap(squares))
     gathered = exchange(normed)
     partial_qkv = product(gathered.reshape(wide, feats), qkv_weight)

time: 62 us -> 55.7 us (0.90)
  local copies, waits for them, and re-layouts: 8.01 us -> 1.82 us
    unnamed x16 -> x22, local copies, waits for them, and re-layouts: 8.01 us -> 1.82 us
where the time goes in v1:
time: 55.7 us; the launch traced here: 55.4 us
  blocking collectives  42.3 us (76%)
  Pallas kernels  6.43 us (12%)
  waiting for transfers between devices  3.29 us (6%)
  local copies, waits for them, and re-layouts  1.82 us (3%)
  between operations  0.77 us (1%)
  starting transfers between devices  0.56 us (1%)
    all_to_all x4, blocking collectives, exchange(): return lax.all_to_all(x, 'wide', split_axis=0, concat_axis=0, tiled=True)  42.3 us
    pallas_call x2, Pallas kernels, product(): pl.pallas_call(product_kernel, out_shape=jax.ShapeDtypeStruct((rows, 1, c...  4.82 us
    ppermute x3, waiting for transfers between devices, swap(): return lax.ppermute(x, 'narrow', [(0, 1), (1, 0)])  3.29 us
    unnamed x22, local copies, waits for them, and re-layouts  1.82 us
  transfers between devices with their start and end apart: 3, of which 3 were waited for; matrix products, arithmetic and copies ran while one was open for 0% of the time, Pallas kernels for 0%

profile of v1, /device:TPU:0, one launch (start us, length us, event | category | flops | bytes accessed | tf_op | source)
XLA Modules:
  0.0 55.4 jit_solution(6210061777405721105)
XLA Ops:
  0.7 0.1 fusion.2
  0.7 0.1 fusion
  0.8 0.1 maximum_bitcast_fusion
  0.8 0.1 maximum_bitcast_fusion.1
  0.9 0.0 copy-start.3
  0.9 0.8 %copy-done.3 = bf16[1,8192]{1,0:T(2,128)(2,1)S(1)} copy-done((bf16[1,8192]{1,0:T(2,128)(2,1)S(1)}, bf16[1,8192]{1,0:T(2,128)(2,1)}, u32[]{:S(2)}) %copy-start.3) | copy-done | bytes 16408
  1.7 0.6 %collective-permute-start = (f32[8,128]{1,0:T(8,128)S(1)}, f32[8,128]{1,0:T(8,128)S(1)}, u32[]{:S(2)}, u32[]{:S(2)}) collective-permute-start(f32[8,128]{1,0:T(8,128)S(1)} %get-tuple-element.15.own_ref), channel_id=1, source_target_pairs={{0,1},{1,0},{2,3},{3,2},{4,5},{5,4},{6,7},{7,6},{8,9},{9,8},{10,11... | collective-permute-start | bytes 12296 | tf_op jit(solution)/shard_map/ppermute | solution.py:136
  2.3 0.8 %collective-permute-done.other_ref = f32[8,128]{1,0:T(8,128)S(1)} collective-permute-done((f32[8,128]{1,0:T(8,128)S(1)}, f32[8,128]{1,0:T(8,128)S(1)}, u32[]{:S(2)}, u32[]{:S(2)}) %collective-permute-start) | collective-permute-done | bytes 4128 | tf_op jit(solution)/shard_map/ppermute | solution.py:136
  3.1 0.0 slice-start
  3.1 0.0 copy-start.5
  3.1 0.9 %copy-done.5 = f32[8192]{0:T(1024)S(1)} copy-done((f32[8192]{0:T(1024)S(1)}, f32[8192]{0:T(1024)}, u32[]{:S(2)}) %copy-start.5) | copy-done | bytes 32792
  4.0 0.0 copy-start
  4.0 0.0 slice-start.1
  4.0 0.0 slice-start.2
  4.0 0.0 slice-start.3
  4.0 0.1 shard_map.74
  4.2 0.0 copy-start.1
  4.2 0.0 copy-start.2
  4.2 0.0 copy-start.4
  4.2 14.5 %all_to_all.20 = bf16[8,64,128]{2,1,0:T(8,128)(2,1)S(1)} all-to-all(bf16[8,64,128]{2,1,0:T(8,128)(2,1)S(1)} %shard_map.74), channel_id=1, replica_groups=mesh['group'=2,'wide'=8,'narrow'=2] {'wide'}, dimensions={0} | all-to-all | bytes 262144 | tf_op jit(solution)/shard_map/all_to_all | solution.py:140
  18.7 0.1 copy.12
  18.8 0.0 copy-done
  18.9 2.5 %shard_map.75 = f32[8,1,1152]{2,1,0:T(1,128)S(1)} custom-call(bf16[8,8192]{1,0:T(8,128)(2,1)S(1)} %bitcast.19, bf16[8192,1152]{1,0:T(8,128)(2,1)S(1)} %copy-done), custom_call_target="tpu_custom_call" | custom-call | flops 150994944 | bytes 18874368 | tf_op jit(solution)/shard_map/pallas_call | solution.py:64
  21.4 9.2 %all_to_all.21.own_ref = f32[8,1,1152]{2,1,0:T(1,128)S(1)} all-to-all(f32[8,1,1152]{2,1,0:T(1,128)S(1)} %shard_map.75), channel_id=1, replica_groups=mesh['group'=2,'wide'=8,'narrow'=2] {'wide'}, dimensions={0} | all-to-all | bytes 73728 | tf_op jit(solution)/shard_map/all_to_all | solution.py:140
  30.6 0.0 collective-permute-start.1
  30.6 1.2 %collective-permute-done.1.other_ref = f32[8,1,1152]{2,1,0:T(1,128)S(1)} collective-permute-done((f32[8,1,1152]{2,1,0:T(1,128)S(1)}, f32[8,1,1152]{2,1,0:T(1,128)S(1)}, u32[]{:S(2)}, u32[]{:S(2)}) %collective-permute-start.1) | collective-permute-done | bytes 36896 | tf_op jit(solution)/shard_map/ppermute | solution.py:136
  31.8 0.0 copy-done.1
  31.8 0.0 copy-done.2
  31.8 0.8 %shard_map.76 = bf16[8,32,128]{2,1,0:T(8,128)(2,1)S(1)} custom-call(s32[1]{0:T(128)} %bitcast.core_ref, s32[1]{0:T(128)S(6)} %copy.14.len_ref, f32[8,1,1152]{2,1,0:T(1,128)S(1)} %all_to_all.21.own_ref, f32[8,1,1152]{2,1,0:T(1,128)S(1)} %collective-permute-done.1.other_ref, f32[2,128]{1,0:T(2,128)S(1)} %pad_maximum_fusion.table_ref, ...), custom_call_target="tpu_custom_call" | custom-call | flops 1000 | bytes 40000000 | tf_op jit(solution)/shard_map/pallas_call | solution.py:184
  32.6 9.3 %all_to_all.22 = bf16[8,32,128]{2,1,0:T(8,128)(2,1)S(1)} all-to-all(bf16[8,32,128]{2,1,0:T(8,128)(2,1)S(1)} %shard_map.76), channel_id=1, replica_groups=mesh['group'=2,'wide'=8,'narrow'=2] {'wide'}, dimensions={0} | all-to-all | bytes 131072 | tf_op jit(solution)/shard_map/all_to_all | solution.py:140
  41.9 0.0 slice-done
  41.9 0.0 slice-done.1
  42.0 0.0 slice-done.2
  42.0 0.0 slice-done.3
  42.0 2.3 %shard_map.77 = f32[8,1,2048]{2,1,0:T(1,128)S(1)} custom-call(bf16[8,4096]{1,0:T(8,128)(2,1)S(1)} %bitcast.20, bf16[4096,2048]{1,0:T(8,128)(2,1)S(1)} %bitcast.18), custom_call_target="tpu_custom_call" | custom-call | flops 134217728 | bytes 16777216 | tf_op jit(solution)/shard_map/pallas_call | solution.py:64
  44.3 9.3 %all_to_all.23.own_ref = f32[8,1,2048]{2,1,0:T(1,128)S(1)} all-to-all(f32[8,1,2048]{2,1,0:T(1,128)S(1)} %shard_map.77), channel_id=1, replica_groups=mesh['group'=2,'wide'=8,'narrow'=2] {'wide'}, dimensions={0} | all-to-all | bytes 131072 | tf_op jit(solution)/shard_map/all_to_all | solution.py:140
  53.5 0.0 collective-permute-start.2
  53.6 1.3 %collective-permute-done.2.other_ref = f32[8,1,2048]{2,1,0:T(1,128)S(1)} collective-permute-done((f32[8,1,2048]{2,1,0:T(1,128)S(1)}, f32[8,1,2048]{2,1,0:T(1,128)S(1)}, u32[]{:S(2)}, u32[]{:S(2)}) %collective-permute-start.2) | collective-permute-done | bytes 65568 | tf_op jit(solution)/shard_map/ppermute | solution.py:136
  54.8 0.0 copy-done.4
  54.8 0.6 %shard_map.78 = f32[1,8192]{1,0:T(1,128)} custom-call(s32[1]{0:T(128)} %bitcast.core_ref, bf16[1,8192]{1,0:T(2,128)(2,1)S(1)} %copy-done.4, f32[8,1,2048]{2,1,0:T(1,128)S(1)} %all_to_all.23.own_ref, f32[8,1,2048]{2,1,0:T(1,128)S(1)} %collective-permute-done.2.other_ref), custom_call_target="tpu_custom_call" | custom-call | flops 1000 | bytes 1000000 | tf_op jit(solution)/shard_map/pallas_call | solution.py:207
  (4 shorter events, 0.1 us)
Async XLA Ops:
  0.9 0.8 %copy-start.3 = (bf16[1,8192]{1,0:T(2,128)(2,1)S(1)}, bf16[1,8192]{1,0:T(2,128)(2,1)}, u32[]{:S(2)}) copy-start(bf16[1,8192]{1,0:T(2,128)(2,1)} %x_ref.1) | copy-start | bytes 49156
  1.7 1.4 %collective-permute-start = (f32[8,128]{1,0:T(8,128)S(1)}, f32[8,128]{1,0:T(8,128)S(1)}, u32[]{:S(2)}, u32[]{:S(2)}) collective-permute-start(f32[8,128]{1,0:T(8,128)S(1)} %get-tuple-element.15.own_ref), channel_id=1, source_target_pairs={{0,1},{1,0},{2,3},{3,2},{4,5},{5,4},{6,7},{7,6},{8,9},{9,8},{10,11... | collective-permute-start | bytes 12296 | tf_op jit(solution)/shard_map/ppermute | solution.py:136
  3.1 38.8 %slice-start = ((s8[16777216]{0:T(1024)(128)(4,1)}), s8[4194304]{0:T(1024)(128)(4,1)S(1)}, s32[]{:S(2)}) async-start(s8[16777216]{0:T(1024)(128)(4,1)} %bitcast.17), calls=%async_computation.4 | async-start | bytes 8388608
  3.1 0.9 %copy-start.5 = (f32[8192]{0:T(1024)S(1)}, f32[8192]{0:T(1024)}, u32[]{:S(2)}) copy-start(f32[8192]{0:T(1024)} %param.8) | copy-start | bytes 98308
  4.0 14.8 %copy-start = (bf16[8192,1152]{1,0:T(8,128)(2,1)S(1)}, bf16[8192,1152]{1,0:T(8,128)(2,1)}, u32[]{:S(2)}) copy-start(bf16[8192,1152]{1,0:T(8,128)(2,1)} %w_ref.2) | copy-start | bytes 56623108
  4.0 37.9 %slice-start.1 = ((s8[16777216]{0:T(1024)(128)(4,1)}), s8[4194304]{0:T(1024)(128)(4,1)S(1)}, s32[]{:S(2)}) async-start(s8[16777216]{0:T(1024)(128)(4,1)} %bitcast.17), calls=%async_computation.5 | async-start | bytes 8388608
  4.0 37.9 %slice-start.2 = ((s8[16777216]{0:T(1024)(128)(4,1)}), s8[4194304]{0:T(1024)(128)(4,1)S(1)}, s32[]{:S(2)}) async-start(s8[16777216]{0:T(1024)(128)(4,1)} %bitcast.17), calls=%async_computation.6 | async-start | bytes 8388608
  4.0 37.9 %slice-start.3 = ((s8[16777216]{0:T(1024)(128)(4,1)}), s8[4194304]{0:T(1024)(128)(4,1)S(1)}, s32[]{:S(2)}) async-start(s8[16777216]{0:T(1024)(128)(4,1)} %bitcast.17), calls=%async_computation.7 | async-start | bytes 8388608
  4.2 27.6 %copy-start.1 = (bf16[1,256,256]{2,1,0:T(8,128)(2,1)S(1)}, bf16[1,256,256]{2,1,0:T(8,128)(2,1)}, u32[]{:S(2)}) copy-start(bf16[1,256,256]{2,1,0:T(8,128)(2,1)} %param.11) | copy-start | bytes 393220
  4.2 27.6 %copy-start.2 = (bf16[1,256,256]{2,1,0:T(8,128)(2,1)S(1)}, bf16[1,256,256]{2,1,0:T(8,128)(2,1)}, u32[]{:S(2)}) copy-start(bf16[1,256,256]{2,1,0:T(8,128)(2,1)} %param.12) | copy-start | bytes 393220
  4.2 50.6 %copy-start.4 = (bf16[1,8192]{1,0:T(2,128)(2,1)S(1)}, bf16[1,8192]{1,0:T(2,128)(2,1)}, u32[]{:S(2)}) copy-start(bf16[1,8192]{1,0:T(2,128)(2,1)} %x_ref.1) | copy-start | bytes 49156
  30.6 1.2 %collective-permute-start.1 = (f32[8,1,1152]{2,1,0:T(1,128)S(1)}, f32[8,1,1152]{2,1,0:T(1,128)S(1)}, u32[]{:S(2)}, u32[]{:S(2)}) collective-permute-start(f32[8,1,1152]{2,1,0:T(1,128)S(1)} %all_to_all.21.own_ref), channel_id=1, source_target_pairs={{0,1},{1,0},{2,3},{3,2},{4,5},{5,4},{6,7},{7,6},{8,9},{9,8},{10,11... | collective-permute-start | bytes 110600 | tf_op jit(solution)/shard_map/ppermute | solution.py:136
  53.5 1.3 %collective-permute-start.2 = (f32[8,1,2048]{2,1,0:T(1,128)S(1)}, f32[8,1,2048]{2,1,0:T(1,128)S(1)}, u32[]{:S(2)}, u32[]{:S(2)}) collective-permute-start(f32[8,1,2048]{2,1,0:T(1,128)S(1)} %all_to_all.23.own_ref), channel_id=1, source_target_pairs={{0,1},{1,0},{2,3},{3,2},{4,5},{5,4},{6,7},{7,6},{8,9},{9,8},{10,11... | collective-permute-start | bytes 196616 | tf_op jit(solution)/shard_map/ppermute | solution.py:136

commit v2 on v1

--- a/solution.py
+++ b/solution.py
@@ -16,7 +16,7 @@
 
 VMEM = pl.BlockSpec(memory_space=pltpu.VMEM)
 SMEM = pl.BlockSpec(memory_space=pltpu.SMEM)
-HBM = pl.BlockSpec(memory_space=pl.ANY)
+HBM = pl.BlockSpec(memory_space=pltpu.HBM)
 
 
 def params(limit):
@@ -36,8 +36,14 @@
     return jnp.stack([jnp.concatenate([cosine, cosine]), jnp.concatenate([-sine, sine])])
 
 
-def square_kernel(x_ref, f_ref, s_ref):
+def square_kernel(x_hbm, g_hbm, f_ref, g_ref, s_ref, x_ref, sems):
     tiles = f_ref.shape[0]
+    x_copy = pltpu.make_async_copy(x_hbm, x_ref, sems.at[0])
+    g_copy = pltpu.make_async_copy(g_hbm, g_ref, sems.at[1])
+    x_copy.start()
+    g_copy.start()
+    x_copy.wait()
+    g_copy.wait()
     for j in range(tiles):
         f_ref[j : j + 1, :] = x_ref[:, j * LANES : (j + 1) * LANES].astype(jnp.float32)
     values = f_ref[...]
@@ -54,16 +60,18 @@
 
 def product_kernel(x_ref, w_ref, o_ref):
     result = jnp.dot(x_ref[...], w_ref[...], preferred_element_type=jnp.float32)
-    for r in range(result.shape[0]):
-        o_ref[r] = result[r : r + 1, :]
-
-
-def product(x, w):
+    copies = o_ref.shape[0] // result.shape[0]
+    for r in range(o_ref.shape[0]):
+        row = r // copies
+        o_ref[r] = result[row : row + 1, :]
+
+
+def product(x, w, copies):
     rows, depth = x.shape
     cols = w.shape[1]
     return pl.pallas_call(
         product_kernel,
-        out_shape=jax.ShapeDtypeStruct((rows, 1, cols), jnp.float32),
+        out_shape=jax.ShapeDtypeStruct((rows * copies, 1, cols), jnp.float32),
         in_specs=[VMEM, VMEM],
         out_specs=VMEM,
         compiler_params=params(4 << 20),
@@ -103,9 +111,9 @@
             o_ref[j, g * share : (g + 1) * share, :] = mixed
 
 
-def direct_kernel(core_ref, len_ref, own_ref, other_ref, table_ref, k_ref, v_ref, o_ref, joined):
-    half = own_ref.shape[0] // 2
-    cols = own_ref.shape[2]
+def direct_kernel(core_ref, len_ref, parts_ref, table_ref, k_ref, v_ref, o_ref, joined):
+    half = parts_ref.shape[0] // 4
+    cols = parts_ref.shape[2]
     groups, slots, _ = joined.shape
     first = core_ref[0] * half
     for b in range(half):
@@ -113,7 +121,7 @@
             piece = b * (cols // LANES) + c
             lanes = slice(c * LANES, (c + 1) * LANES)
             joined[piece // slots, piece % slots : piece % slots + 1, :] = (
-                own_ref[first + b, :, lanes] + other_ref[first + b, :, lanes]
+                parts_ref[2 * (first + b), :, lanes] + parts_ref[2 * (first + b) + 1, :, lanes]
             )
     attend_kernel(joined, len_ref[0], table_ref[...], k_ref, v_ref, o_ref)
 
@@ -136,29 +144,32 @@
     return lax.ppermute(x, "narrow", [(0, 1), (1, 0)])
 
 
-def exchange(x):
-    return lax.all_to_all(x, "wide", split_axis=0, concat_axis=0, tiled=True)
+def exchange(x, axes="wide"):
+    return lax.all_to_all(x, axes, split_axis=0, concat_axis=0, tiled=True)
 
 
 def body(hidden_in, norm_gain, qkv_weight, out_weight, cache_keys, cache_values, cache_lengths):
     wide = lax.axis_size("wide")
     core = lax.axis_index("narrow").astype(jnp.int32).reshape(1)
-    table = rope_tables(cache_lengths)
-    lengths = cache_lengths
-    hidden_in, core, table, lengths = lax.optimization_barrier((hidden_in, core, table, lengths))
+    hidden_in, core = lax.optimization_barrier((hidden_in, core))
     feats = hidden_in.shape[1]
     tiles = feats // LANES
-    values, squares = pl.pallas_call(
+    values, gain, squares = pl.pallas_call(
         square_kernel,
         out_shape=(
             jax.ShapeDtypeStruct((tiles, LANES), jnp.float32),
+            jax.ShapeDtypeStruct((tiles, LANES), jnp.float32),
             jax.ShapeDtypeStruct((8, LANES), jnp.float32),
         ),
-        in_specs=[VMEM],
-        out_specs=(VMEM, VMEM),
+        in_specs=[HBM, HBM],
+        out_specs=(VMEM, VMEM, VMEM),
+        scratch_shapes=[pltpu.VMEM(hidden_in.shape, hidden_in.dtype), pltpu.SemaphoreType.DMA((2,))],
         compiler_params=params(4 << 20),
         cost_estimate=cost(1000, 64_000),
-    )(hidden_in)
+    )(hidden_in, norm_gain.reshape(tiles, LANES))
+    squares, lengths = lax.optimization_barrier((squares, cache_lengths))
+    table = rope_tables(lengths)
+    others, table = lax.optimization_barrier((swap(squares), table))
     normed = pl.pallas_call(
         norm_kernel,
         out_shape=jax.ShapeDtypeStruct((wide, tiles, LANES), jnp.bfloat16),
@@ -166,11 +177,10 @@
         out_specs=VMEM,
         compiler_params=params(4 << 20),
         cost_estimate=cost(40_000_000_000, 40_000_000),
-    )(values, norm_gain.reshape(tiles, LANES), squares, swap(squares))
+    )(values, gain, squares, others)
     gathered = exchange(normed)
-    partial_qkv = product(gathered.reshape(wide, feats), qkv_weight)
-    moved = exchange(partial_qkv)
-    other = swap(moved)
+    partial_qkv = product(gathered.reshape(wide, feats), qkv_weight, 2)
+    moved = exchange(partial_qkv, ("wide", "narrow"))
     capacity = cache_keys.shape[1]
     groups = cache_keys.shape[2] // HD
     keys = cache_keys.reshape(capacity, groups * HD)
@@ -184,15 +194,16 @@
         mixed = pl.pallas_call(
             direct_kernel,
             out_shape=mixed_shape,
-            in_specs=[SMEM, SMEM, VMEM, VMEM, VMEM, VMEM, VMEM],
+            in_specs=[SMEM, SMEM, VMEM, VMEM, VMEM, VMEM],
             out_specs=VMEM,
             scratch_shapes=[pltpu.VMEM((groups, slots, HD), jnp.float32)],
             compiler_params=params(4 << 20),
             cost_estimate=cost(1000, 40_000_000),
-        )(core, lengths, moved, other, table, keys, cached)
+        )(core, lengths, moved, table, keys, cached)
     else:
         first = core[0] * (wide // 2)
-        joined = lax.dynamic_slice_in_dim(moved + other, first, wide // 2, 0)
+        joined = jnp.sum(moved.reshape(wide, 2, block), axis=1)
+        joined = lax.dynamic_slice_in_dim(joined, first, wide // 2, 0)
         mixed = pl.pallas_call(
             given_kernel,
             out_shape=mixed_shape,
@@ -202,7 +213,7 @@
             cost_estimate=cost(1000, 40_000_000),
         )(lengths, joined.reshape(groups, slots, HD), table, keys, cached)
     spread = exchange(mixed)
-    partial_out = product(spread.reshape(wide, depth), out_weight)
+    partial_out = product(spread.reshape(wide, depth), out_weight, 1)
     added = exchange(partial_out)
     return pl.pallas_call(
         add_kernel,

time: 55.7 us -> 54.1 us (0.971)
  waiting for transfers between devices: 3.29 us -> 1.25 us
    ppermute x3 -> x2, waiting for transfers between devices: 3.29 us -> 1.25 us  [swap(): return lax.ppermute(x, 'narrow', [(0, 1), (1, 0)])]
  transfers between devices with their start and end apart: 3 -> 2, of which waited for: 3 -> 1; matrix products, arithmetic and copies ran while one was open for 0% -> 0% of each run, Pallas kernels for 0% -> 0%
where the time goes in v2:
time: 54.1 us; the launch traced here: 53.8 us
  blocking collectives  42.7 us (79%)
  Pallas kernels  6.5 us (12%)
  local copies, waits for them, and re-layouts  1.68 us (3%)
  waiting for transfers between devices  1.25 us (2%)
  between operations  0.82 us (2%)
  starting transfers between devices  0.56 us (1%)
    all_to_all x4, blocking collectives, exchange(): return lax.all_to_all(x, axes, split_axis=0, concat_axis=0, tiled=True)  42.7 us
    pallas_call x2, Pallas kernels, product(): pl.pallas_call(product_kernel, out_shape=jax.ShapeDtypeStruct((rows * cop...  4.82 us
    unnamed x22, local copies, waits for them, and re-layouts  1.68 us
    ppermute x2, waiting for transfers between devices, swap(): return lax.ppermute(x, 'narrow', [(0, 1), (1, 0)])  1.25 us
  transfers between devices with their start and end apart: 2, of which 1 were waited for; matrix products, arithmetic and copies ran while one was open for 0% of the time, Pallas kernels for 0%

profile of v2, /device:TPU:0, one launch (start us, length us, event | category | flops | bytes accessed | tf_op | source)
XLA Modules:
  0.0 53.8 jit_solution(4617737758408287828)
XLA Ops:
  0.0 0.0 copy-start.3
  0.0 0.8 %copy-done.3 = bf16[1,8192]{1,0:T(2,128)(2,1)S(1)} copy-done((bf16[1,8192]{1,0:T(2,128)(2,1)S(1)}, bf16[1,8192]{1,0:T(2,128)(2,1)}, u32[]{:S(2)}) %copy-start.3) | copy-done | bytes 16408
  0.8 0.0 copy-start.5
  0.8 0.8 %copy-done.5 = f32[8192]{0:T(1024)S(1)} copy-done((f32[8192]{0:T(1024)S(1)}, f32[8192]{0:T(1024)}, u32[]{:S(2)}) %copy-start.5) | copy-done | bytes 32792
  1.5 0.1 shard_map.73
  1.6 0.6 %collective-permute-start = (f32[8,128]{1,0:T(8,128)S(1)}, f32[8,128]{1,0:T(8,128)S(1)}, u32[]{:S(2)}, u32[]{:S(2)}) collective-permute-start(f32[8,128]{1,0:T(8,128)S(1)} %get-tuple-element.20.own_ref), channel_id=1, source_target_pairs={{0,1},{1,0},{2,3},{3,2},{4,5},{5,4},{6,7},{7,6},{8,9},{9,8},{10,11... | collective-permute-start | bytes 12296 | tf_op jit(solution)/shard_map/ppermute | solution.py:144
  2.8 0.1 fusion.2
  2.9 0.1 fusion
  3.0 0.1 maximum_bitcast_fusion
  3.0 0.1 maximum_bitcast_fusion.1
  3.1 0.0 collective-permute-done.other_ref
  3.1 0.0 slice-start
  3.1 0.0 copy-start
  3.1 0.0 slice-start.1
  3.2 0.0 slice-start.2
  3.2 0.0 slice-start.3
  3.2 0.1 shard_map.74
  3.3 0.0 copy-start.1
  3.3 0.0 copy-start.2
  3.3 0.0 copy-start.4
  3.4 14.5 %all_to_all.20 = bf16[8,64,128]{2,1,0:T(8,128)(2,1)S(1)} all-to-all(bf16[8,64,128]{2,1,0:T(8,128)(2,1)S(1)} %shard_map.74), channel_id=1, replica_groups=mesh['group'=2,'wide'=8,'narrow'=2] {'wide'}, dimensions={0} | all-to-all | bytes 262144 | tf_op jit(solution)/shard_map/all_to_all | solution.py:148
  17.9 0.1 copy.12
  18.0 0.0 copy-done
  18.0 2.5 %shard_map.75 = f32[16,1,1152]{2,1,0:T(1,128)S(1)} custom-call(bf16[8,8192]{1,0:T(8,128)(2,1)S(1)} %bitcast.19, bf16[8192,1152]{1,0:T(8,128)(2,1)S(1)} %copy-done), custom_call_target="tpu_custom_call" | custom-call | flops 150994944 | bytes 18874368 | tf_op jit(solution)/shard_map/pallas_call | solution.py:72
  20.5 9.6 %all_to_all.21.parts_ref = f32[16,1,1152]{2,1,0:T(1,128)S(1)} all-to-all(f32[16,1,1152]{2,1,0:T(1,128)S(1)} %shard_map.75), channel_id=1, replica_groups=mesh['group'=2,'wide'=8,'narrow'=2] {'wide','narrow'}, dimensions={0} | all-to-all | bytes 147456 | tf_op jit(solution)/shard_map/all_to_all | solution.py:148
  30.1 0.0 copy-done.1
  30.1 0.0 copy-done.2
  30.1 0.8 %shard_map.76 = bf16[8,32,128]{2,1,0:T(8,128)(2,1)S(1)} custom-call(s32[1]{0:T(128)} %bitcast.core_ref, s32[1]{0:T(128)S(6)} %copy.14.len_ref, f32[16,1,1152]{2,1,0:T(1,128)S(1)} %all_to_all.21.parts_ref, f32[2,128]{1,0:T(2,128)S(1)} %pad_maximum_fusion.table_ref, bf16[256,256]{1,0:T(8,128)(2,1)S(1)} %bitcast.21, bf16[256,256]{1,0:T(8,128)(2,1)S(1)} %bitcast.22), custom_call_target="tpu_custom_call" | custom-call | flops 1000 | bytes 40000000 | tf_op jit(solution)/shard_map/pallas_call | solution.py:194
  30.9 9.3 %all_to_all.22 = bf16[8,32,128]{2,1,0:T(8,128)(2,1)S(1)} all-to-all(bf16[8,32,128]{2,1,0:T(8,128)(2,1)S(1)} %shard_map.76), channel_id=1, replica_groups=mesh['group'=2,'wide'=8,'narrow'=2] {'wide'}, dimensions={0} | all-to-all | bytes 131072 | tf_op jit(solution)/shard_map/all_to_all | solution.py:148
  40.3 0.0 slice-done
  40.3 0.0 slice-done.1
  40.3 0.0 slice-done.2
  40.3 0.0 slice-done.3
  40.3 2.3 %shard_map.77 = f32[8,1,2048]{2,1,0:T(1,128)S(1)} custom-call(bf16[8,4096]{1,0:T(8,128)(2,1)S(1)} %bitcast.20, bf16[4096,2048]{1,0:T(8,128)(2,1)S(1)} %bitcast.18), custom_call_target="tpu_custom_call" | custom-call | flops 134217728 | bytes 16777216 | tf_op jit(solution)/shard_map/pallas_call | solution.py:72
  42.6 9.3 %all_to_all.23.own_ref = f32[8,1,2048]{2,1,0:T(1,128)S(1)} all-to-all(f32[8,1,2048]{2,1,0:T(1,128)S(1)} %shard_map.77), channel_id=1, replica_groups=mesh['group'=2,'wide'=8,'narrow'=2] {'wide'}, dimensions={0} | all-to-all | bytes 131072 | tf_op jit(solution)/shard_map/all_to_all | solution.py:148
  51.9 0.0 collective-permute-start.1
  51.9 1.3 %collective-permute-done.1.other_ref = f32[8,1,2048]{2,1,0:T(1,128)S(1)} collective-permute-done((f32[8,1,2048]{2,1,0:T(1,128)S(1)}, f32[8,1,2048]{2,1,0:T(1,128)S(1)}, u32[]{:S(2)}, u32[]{:S(2)}) %collective-permute-start.1) | collective-permute-done | bytes 65568 | tf_op jit(solution)/shard_map/ppermute | solution.py:144
  53.1 0.0 copy-done.4
  53.1 0.6 %shard_map.78 = f32[1,8192]{1,0:T(1,128)} custom-call(s32[1]{0:T(128)} %bitcast.core_ref, bf16[1,8192]{1,0:T(2,128)(2,1)S(1)} %copy-done.4, f32[8,1,2048]{2,1,0:T(1,128)S(1)} %all_to_all.23.own_ref, f32[8,1,2048]{2,1,0:T(1,128)S(1)} %collective-permute-done.1.other_ref), custom_call_target="tpu_custom_call" | custom-call | flops 1000 | bytes 1000000 | tf_op jit(solution)/shard_map/pallas_call | solution.py:218
  (3 shorter events, 0.0 us)
Async XLA Ops:
  0.0 0.8 %copy-start.3 = (bf16[1,8192]{1,0:T(2,128)(2,1)S(1)}, bf16[1,8192]{1,0:T(2,128)(2,1)}, u32[]{:S(2)}) copy-start(bf16[1,8192]{1,0:T(2,128)(2,1)} %x_ref) | copy-start | bytes 49156
  0.8 0.8 %copy-start.5 = (f32[8192]{0:T(1024)S(1)}, f32[8192]{0:T(1024)}, u32[]{:S(2)}) copy-start(f32[8192]{0:T(1024)} %param.8) | copy-start | bytes 98308
  1.6 1.5 %collective-permute-start = (f32[8,128]{1,0:T(8,128)S(1)}, f32[8,128]{1,0:T(8,128)S(1)}, u32[]{:S(2)}, u32[]{:S(2)}) collective-permute-start(f32[8,128]{1,0:T(8,128)S(1)} %get-tuple-element.20.own_ref), channel_id=1, source_target_pairs={{0,1},{1,0},{2,3},{3,2},{4,5},{5,4},{6,7},{7,6},{8,9},{9,8},{10,11... | collective-permute-start | bytes 12296 | tf_op jit(solution)/shard_map/ppermute | solution.py:144
  3.1 37.1 %slice-start = ((s8[16777216]{0:T(1024)(128)(4,1)}), s8[4194304]{0:T(1024)(128)(4,1)S(1)}, s32[]{:S(2)}) async-start(s8[16777216]{0:T(1024)(128)(4,1)} %bitcast.17), calls=%async_computation.4 | async-start | bytes 8388608
  3.1 14.8 %copy-start = (bf16[8192,1152]{1,0:T(8,128)(2,1)S(1)}, bf16[8192,1152]{1,0:T(8,128)(2,1)}, u32[]{:S(2)}) copy-start(bf16[8192,1152]{1,0:T(8,128)(2,1)} %w_ref.2) | copy-start | bytes 56623108
  3.1 37.1 %slice-start.1 = ((s8[16777216]{0:T(1024)(128)(4,1)}), s8[4194304]{0:T(1024)(128)(4,1)S(1)}, s32[]{:S(2)}) async-start(s8[16777216]{0:T(1024)(128)(4,1)} %bitcast.17), calls=%async_computation.5 | async-start | bytes 8388608
  3.2 37.1 %slice-start.2 = ((s8[16777216]{0:T(1024)(128)(4,1)}), s8[4194304]{0:T(1024)(128)(4,1)S(1)}, s32[]{:S(2)}) async-start(s8[16777216]{0:T(1024)(128)(4,1)} %bitcast.17), calls=%async_computation.6 | async-start | bytes 8388608
  3.2 37.1 %slice-start.3 = ((s8[16777216]{0:T(1024)(128)(4,1)}), s8[4194304]{0:T(1024)(128)(4,1)S(1)}, s32[]{:S(2)}) async-start(s8[16777216]{0:T(1024)(128)(4,1)} %bitcast.17), calls=%async_computation.7 | async-start | bytes 8388608
  3.3 26.8 %copy-start.1 = (bf16[1,256,256]{2,1,0:T(8,128)(2,1)S(1)}, bf16[1,256,256]{2,1,0:T(8,128)(2,1)}, u32[]{:S(2)}) copy-start(bf16[1,256,256]{2,1,0:T(8,128)(2,1)} %param.11) | copy-start | bytes 393220
  3.3 26.8 %copy-start.2 = (bf16[1,256,256]{2,1,0:T(8,128)(2,1)S(1)}, bf16[1,256,256]{2,1,0:T(8,128)(2,1)}, u32[]{:S(2)}) copy-start(bf16[1,256,256]{2,1,0:T(8,128)(2,1)} %param.12) | copy-start | bytes 393220
  3.3 49.8 %copy-start.4 = (bf16[1,8192]{1,0:T(2,128)(2,1)S(1)}, bf16[1,8192]{1,0:T(2,128)(2,1)}, u32[]{:S(2)}) copy-start(bf16[1,8192]{1,0:T(2,128)(2,1)} %x_ref) | copy-start | bytes 49156
  51.9 1.3 %collective-permute-start.1 = (f32[8,1,2048]{2,1,0:T(1,128)S(1)}, f32[8,1,2048]{2,1,0:T(1,128)S(1)}, u32[]{:S(2)}, u32[]{:S(2)}) collective-permute-start(f32[8,1,2048]{2,1,0:T(1,128)S(1)} %all_to_all.23.own_ref), channel_id=1, source_target_pairs={{0,1},{1,0},{2,3},{3,2},{4,5},{5,4},{6,7},{7,6},{8,9},{9,8},{10,11... | collective-permute-start | bytes 196616 | tf_op jit(solution)/shard_map/ppermute | solution.py:144

commit v3 on v2

--- a/solution.py
+++ b/solution.py
@@ -16,7 +16,6 @@
 
 VMEM = pl.BlockSpec(memory_space=pltpu.VMEM)
 SMEM = pl.BlockSpec(memory_space=pltpu.SMEM)
-HBM = pl.BlockSpec(memory_space=pltpu.HBM)
 
 
 def params(limit):
@@ -36,14 +35,8 @@
     return jnp.stack([jnp.concatenate([cosine, cosine]), jnp.concatenate([-sine, sine])])
 
 
-def square_kernel(x_hbm, g_hbm, f_ref, g_ref, s_ref, x_ref, sems):
+def square_kernel(x_ref, f_ref, s_ref):
     tiles = f_ref.shape[0]
-    x_copy = pltpu.make_async_copy(x_hbm, x_ref, sems.at[0])
-    g_copy = pltpu.make_async_copy(g_hbm, g_ref, sems.at[1])
-    x_copy.start()
-    g_copy.start()
-    x_copy.wait()
-    g_copy.wait()
     for j in range(tiles):
         f_ref[j : j + 1, :] = x_ref[:, j * LANES : (j + 1) * LANES].astype(jnp.float32)
     values = f_ref[...]
@@ -60,18 +53,22 @@
 
 def product_kernel(x_ref, w_ref, o_ref):
     result = jnp.dot(x_ref[...], w_ref[...], preferred_element_type=jnp.float32)
-    copies = o_ref.shape[0] // result.shape[0]
-    for r in range(o_ref.shape[0]):
-        row = r // copies
-        o_ref[r] = result[row : row + 1, :]
-
-
-def product(x, w, copies):
+    rows = result.shape[0]
+    lines, cols = o_ref.shape[1:]
+    copies = o_ref.shape[0] // rows
+    for r in range(rows):
+        row = [result[r : r + 1, i * cols : (i + 1) * cols] for i in range(lines)]
+        block = jnp.concatenate(row, axis=0).astype(o_ref.dtype)
+        for j in range(copies):
+            o_ref[r * copies + j] = block
+
+
+def product(x, w, copies, lines, dtype):
     rows, depth = x.shape
     cols = w.shape[1]
     return pl.pallas_call(
         product_kernel,
-        out_shape=jax.ShapeDtypeStruct((rows * copies, 1, cols), jnp.float32),
+        out_shape=jax.ShapeDtypeStruct((rows * copies, lines, cols // lines), dtype),
         in_specs=[VMEM, VMEM],
         out_specs=VMEM,
         compiler_params=params(4 << 20),
@@ -130,14 +127,16 @@
     attend_kernel(joined_ref, len_ref[0], table_ref[...], k_ref, v_ref, o_ref)
 
 
-def add_kernel(core_ref, x_ref, own_ref, other_ref, o_ref):
-    half = own_ref.shape[0] // 2
-    cols = own_ref.shape[2]
+def add_kernel(core_ref, x_ref, parts_ref, o_ref):
+    half = parts_ref.shape[0] // 4
+    lines, cols = parts_ref.shape[1:]
     first = core_ref[0] * half
     for b in range(half):
-        lanes = slice(b * cols, (b + 1) * cols)
-        added = own_ref[first + b] + other_ref[first + b]
-        o_ref[:, lanes] = x_ref[:, lanes].astype(jnp.float32) + added
+        one = parts_ref[2 * (first + b)].astype(jnp.float32)
+        added = one + parts_ref[2 * (first + b) + 1].astype(jnp.float32)
+        for i in range(lines):
+            lanes = slice((b * lines + i) * cols, (b * lines + i + 1) * cols)
+            o_ref[:, lanes] = x_ref[:, lanes].astype(jnp.float32) + added[i : i + 1, :]
 
 
 def swap(x):
@@ -154,19 +153,17 @@
     hidden_in, core = lax.optimization_barrier((hidden_in, core))
     feats = hidden_in.shape[1]
     tiles = feats // LANES
-    values, gain, squares = pl.pallas_call(
+    values, squares = pl.pallas_call(
         square_kernel,
         out_shape=(
             jax.ShapeDtypeStruct((tiles, LANES), jnp.float32),
-            jax.ShapeDtypeStruct((tiles, LANES), jnp.float32),
             jax.ShapeDtypeStruct((8, LANES), jnp.float32),
         ),
-        in_specs=[HBM, HBM],
-        out_specs=(VMEM, VMEM, VMEM),
-        scratch_shapes=[pltpu.VMEM(hidden_in.shape, hidden_in.dtype), pltpu.SemaphoreType.DMA((2,))],
-        compiler_params=params(4 << 20),
-        cost_estimate=cost(1000, 64_000),
-    )(hidden_in, norm_gain.reshape(tiles, LANES))
+        in_specs=[VMEM],
+        out_specs=(VMEM, VMEM),
+        compiler_params=params(4 << 20),
+        cost_estimate=cost(40_000_000_000, 64_000),
+    )(hidden_in)
     squares, lengths = lax.optimization_barrier((squares, cache_lengths))
     table = rope_tables(lengths)
     others, table = lax.optimization_barrier((swap(squares), table))
@@ -177,9 +174,9 @@
         out_specs=VMEM,
         compiler_params=params(4 << 20),
         cost_estimate=cost(40_000_000_000, 40_000_000),
-    )(values, gain, squares, others)
+    )(values, norm_gain.reshape(tiles, LANES), squares, others)
     gathered = exchange(normed)
-    partial_qkv = product(gathered.reshape(wide, feats), qkv_weight, 2)
+    partial_qkv = product(gathered.reshape(wide, feats), qkv_weight, 2, 1, jnp.float32)
     moved = exchange(partial_qkv, ("wide", "narrow"))
     capacity = cache_keys.shape[1]
     groups = cache_keys.shape[2] // HD
@@ -213,16 +210,17 @@
             cost_estimate=cost(1000, 40_000_000),
         )(lengths, joined.reshape(groups, slots, HD), table, keys, cached)
     spread = exchange(mixed)
-    partial_out = product(spread.reshape(wide, depth), out_weight, 1)
-    added = exchange(partial_out)
+    lines = 2 if out_weight.shape[1] % (2 * LANES) == 0 else 1
+    partial_out = product(spread.reshape(wide, depth), out_weight, 2, lines, jnp.bfloat16)
+    parts = exchange(partial_out, ("wide", "narrow"))
     return pl.pallas_call(
         add_kernel,
         out_shape=jax.ShapeDtypeStruct((1, feats), jnp.float32),
-        in_specs=[SMEM, VMEM, VMEM, VMEM],
+        in_specs=[SMEM, VMEM, VMEM],
         out_specs=VMEM,
         compiler_params=params(4 << 20),
         cost_estimate=cost(1000, 1_000_000),
-    )(core, hidden_in, added, swap(added))
+    )(core, hidden_in, parts)
 
 
 def solution(mesh):

time: 54.1 us -> 52.6 us (0.972)
  waiting for transfers between devices: 1.25 us -> 0.01 us
  local copies, waits for them, and re-layouts: 1.68 us -> 0.94 us
    ppermute x2 -> x1, waiting for transfers between devices: 1.25 us -> 0.01 us  [swap(): return lax.ppermute(x, 'narrow', [(0, 1), (1, 0)])]
    unnamed x22 -> x30, local copies, waits for them, and re-layouts: 1.68 us -> 0.94 us
  transfers between devices with their start and end apart: 2 -> 1, of which waited for: 1 -> 0; matrix products, arithmetic and copies ran while one was open for 0% -> 1% of each run, Pallas kernels for 0% -> 0%
where the time goes in v3:
time: 52.6 us; the launch traced here: 52.4 us
  blocking collectives  43 us (82%)
  Pallas kernels  6.46 us (12%)
  between operations  1.18 us (2%)
  local copies, waits for them, and re-layouts  0.94 us (2%)
  starting transfers between devices  0.56 us (1%)
    all_to_all x4, blocking collectives, exchange(): return lax.all_to_all(x, axes, split_axis=0, concat_axis=0, tiled=True)  43 us
    pallas_call x2, Pallas kernels, product(): pl.pallas_call(product_kernel, out_shape=jax.ShapeDtypeStruct((rows * cop...  4.84 us
  transfers between devices with their start and end apart: 1, of which 0 were waited for; matrix products, arithmetic and copies ran while one was open for 1% of the time, Pallas kernels for 0%

profile of v3, /device:TPU:0, one launch (start us, length us, event | category | flops | bytes accessed | tf_op | source)
XLA Modules:
  0.0 52.4 jit_solution(7551017462853326320)
XLA Ops:
  0.0 0.0 copy-start.2
  0.0 0.8 %copy-done.2 = bf16[1,8192]{1,0:T(2,128)(2,1)S(1)} copy-done((bf16[1,8192]{1,0:T(2,128)(2,1)S(1)}, bf16[1,8192]{1,0:T(2,128)(2,1)}, u32[]{:S(2)}) %copy-start.2) | copy-done | bytes 16408
  0.8 0.0 copy-start.4
  0.8 0.0 slice-start
  0.8 0.0 slice-start.1
  0.8 0.0 slice-start.2
  0.8 0.6 %collective-permute-start = (f32[8,128]{1,0:T(8,128)S(1)}, f32[8,128]{1,0:T(8,128)S(1)}, u32[]{:S(2)}, u32[]{:S(2)}) collective-permute-start(f32[8,128]{1,0:T(8,128)S(1)} %get-tuple-element.18.own_ref), channel_id=1, source_target_pairs={{0,1},{1,0},{2,3},{3,2},{4,5},{5,4},{6,7},{7,6},{8,9},{9,8},{10,11... | collective-permute-start | bytes 12296 | tf_op jit(solution)/shard_map/ppermute | solution.py:143
  2.3 0.1 fusion.2
  2.4 0.1 fusion
  2.4 0.1 maximum_bitcast_fusion
  2.5 0.1 maximum_bitcast_fusion.1
  2.6 0.0 collective-permute-done.other_ref
  2.6 0.0 slice-start.5
  2.6 0.0 copy-done.4
  2.6 0.0 slice-start.3
  2.6 0.0 slice-start.4
  2.7 0.0 slice-start.6
  2.7 0.0 slice-start.7
  2.7 0.0 slice-start.8
  2.7 0.1 shard_map.74
  2.8 0.0 copy-start
  2.8 0.0 copy-start.1
  2.9 0.0 copy-start.3
  2.9 14.6 %all_to_all.20 = bf16[8,64,128]{2,1,0:T(8,128)(2,1)S(1)} all-to-all(bf16[8,64,128]{2,1,0:T(8,128)(2,1)S(1)} %shard_map.74), channel_id=1, replica_groups=mesh['group'=2,'wide'=8,'narrow'=2] {'wide'}, dimensions={0} | all-to-all | bytes 262144 | tf_op jit(solution)/shard_map/all_to_all | solution.py:147
  17.5 0.1 copy.12
  17.6 0.0 slice-done
  17.6 0.0 slice-done.1
  17.6 0.0 slice-done.2
  17.6 0.0 slice-done.3
  17.6 0.0 slice-done.4
  17.6 2.5 %shard_map.75 = f32[16,1,1152]{2,1,0:T(1,128)S(1)} custom-call(bf16[8,8192]{1,0:T(8,128)(2,1)S(1)} %bitcast.21, bf16[8192,1152]{1,0:T(8,128)(2,1)S(1)} %bitcast.18), custom_call_target="tpu_custom_call" | custom-call | flops 150994944 | bytes 18874368 | tf_op jit(solution)/shard_map/pallas_call | solution.py:69
  20.2 9.6 %all_to_all.21.parts_ref = f32[16,1,1152]{2,1,0:T(1,128)S(1)} all-to-all(f32[16,1,1152]{2,1,0:T(1,128)S(1)} %shard_map.75), channel_id=1, replica_groups=mesh['group'=2,'wide'=8,'narrow'=2] {'wide','narrow'}, dimensions={0} | all-to-all | bytes 147456 | tf_op jit(solution)/shard_map/all_to_all | solution.py:147
  29.8 0.0 copy-done
  29.8 0.0 copy-done.1
  29.8 0.8 %shard_map.76 = bf16[8,32,128]{2,1,0:T(8,128)(2,1)S(1)} custom-call(s32[1]{0:T(128)} %bitcast.core_ref, s32[1]{0:T(128)S(6)} %copy.14.len_ref, f32[16,1,1152]{2,1,0:T(1,128)S(1)} %all_to_all.21.parts_ref, f32[2,128]{1,0:T(2,128)S(1)} %pad_maximum_fusion.table_ref, bf16[256,256]{1,0:T(8,128)(2,1)S(1)} %bitcast.23, bf16[256,256]{1,0:T(8,128)(2,1)S(1)} %bitcast.24), custom_call_target="tpu_custom_call" | custom-call | flops 1000 | bytes 40000000 | tf_op jit(solution)/shard_map/pallas_call | solution.py:191
  30.6 9.3 %all_to_all.22 = bf16[8,32,128]{2,1,0:T(8,128)(2,1)S(1)} all-to-all(bf16[8,32,128]{2,1,0:T(8,128)(2,1)S(1)} %shard_map.76), channel_id=1, replica_groups=mesh['group'=2,'wide'=8,'narrow'=2] {'wide'}, dimensions={0} | all-to-all | bytes 131072 | tf_op jit(solution)/shard_map/all_to_all | solution.py:147
  39.9 0.0 slice-done.5
  39.9 0.0 slice-done.6
  39.9 0.0 slice-done.7
  39.9 0.0 slice-done.8
  39.9 2.3 %shard_map.77 = bf16[16,2,1024]{2,1,0:T(2,128)(2,1)S(1)} custom-call(bf16[8,4096]{1,0:T(8,128)(2,1)S(1)} %bitcast.22, bf16[4096,2048]{1,0:T(8,128)(2,1)S(1)} %bitcast.20), custom_call_target="tpu_custom_call" | custom-call | flops 134217728 | bytes 16777216 | tf_op jit(solution)/shard_map/pallas_call | solution.py:69
  42.2 9.5 %all_to_all.23.parts_ref = bf16[16,2,1024]{2,1,0:T(2,128)(2,1)S(1)} all-to-all(bf16[16,2,1024]{2,1,0:T(2,128)(2,1)S(1)} %shard_map.77), channel_id=1, replica_groups=mesh['group'=2,'wide'=8,'narrow'=2] {'wide','narrow'}, dimensions={0} | all-to-all | bytes 131072 | tf_op jit(solution)/shard_map/all_to_all | solution.py:147
  51.7 0.0 copy-done.3
  51.7 0.6 %shard_map.78 = f32[1,8192]{1,0:T(1,128)} custom-call(s32[1]{0:T(128)} %bitcast.core_ref, bf16[1,8192]{1,0:T(2,128)(2,1)S(1)} %copy-done.3, bf16[16,2,1024]{2,1,0:T(2,128)(2,1)S(1)} %all_to_all.23.parts_ref), custom_call_target="tpu_custom_call" | custom-call | flops 1000 | bytes 1000000 | tf_op jit(solution)/shard_map/pallas_call | solution.py:216
  (5 shorter events, 0.1 us)
Async XLA Ops:
  0.0 0.8 %copy-start.2 = (bf16[1,8192]{1,0:T(2,128)(2,1)S(1)}, bf16[1,8192]{1,0:T(2,128)(2,1)}, u32[]{:S(2)}) copy-start(bf16[1,8192]{1,0:T(2,128)(2,1)} %x_ref.1) | copy-start | bytes 49156
  0.8 1.9 %copy-start.4 = (f32[8192]{0:T(1024)S(1)}, f32[8192]{0:T(1024)}, u32[]{:S(2)}) copy-start(f32[8192]{0:T(1024)} %param.8) | copy-start | bytes 98308
  0.8 16.8 %slice-start = ((s8[18874368]{0:T(1024)(128)(4,1)}), s8[4194304]{0:T(1024)(128)(4,1)S(1)}, s32[]{:S(2)}) async-start(s8[18874368]{0:T(1024)(128)(4,1)} %bitcast.17), calls=%async_computation.4 | async-start | bytes 8388608
  0.8 16.8 %slice-start.1 = ((s8[18874368]{0:T(1024)(128)(4,1)}), s8[4194304]{0:T(1024)(128)(4,1)S(1)}, s32[]{:S(2)}) async-start(s8[18874368]{0:T(1024)(128)(4,1)} %bitcast.17), calls=%async_computation.5 | async-start | bytes 8388608
  0.8 16.8 %slice-start.2 = ((s8[18874368]{0:T(1024)(128)(4,1)}), s8[4194304]{0:T(1024)(128)(4,1)S(1)}, s32[]{:S(2)}) async-start(s8[18874368]{0:T(1024)(128)(4,1)} %bitcast.17), calls=%async_computation.6 | async-start | bytes 8388608
  0.8 1.8 %collective-permute-start = (f32[8,128]{1,0:T(8,128)S(1)}, f32[8,128]{1,0:T(8,128)S(1)}, u32[]{:S(2)}, u32[]{:S(2)}) collective-permute-start(f32[8,128]{1,0:T(8,128)S(1)} %get-tuple-element.18.own_ref), channel_id=1, source_target_pairs={{0,1},{1,0},{2,3},{3,2},{4,5},{5,4},{6,7},{7,6},{8,9},{9,8},{10,11... | collective-permute-start | bytes 12296 | tf_op jit(solution)/shard_map/ppermute | solution.py:143
  2.6 37.3 %slice-start.5 = ((s8[16777216]{0:T(1024)(128)(4,1)}), s8[4194304]{0:T(1024)(128)(4,1)S(1)}, s32[]{:S(2)}) async-start(s8[16777216]{0:T(1024)(128)(4,1)} %bitcast.19), calls=%async_computation.9 | async-start | bytes 8388608
  2.6 15.0 %slice-start.3 = ((s8[18874368]{0:T(1024)(128)(4,1)}), s8[4194304]{0:T(1024)(128)(4,1)S(1)}, s32[]{:S(2)}) async-start(s8[18874368]{0:T(1024)(128)(4,1)} %bitcast.17), calls=%async_computation.7 | async-start | bytes 8388608
  2.6 15.0 %slice-start.4 = ((s8[18874368]{0:T(1024)(128)(4,1)}), s8[2097152]{0:T(1024)(128)(4,1)S(1)}, s32[]{:S(2)}) async-start(s8[18874368]{0:T(1024)(128)(4,1)} %bitcast.17), calls=%async_computation.8 | async-start | bytes 4194304
  2.7 37.3 %slice-start.6 = ((s8[16777216]{0:T(1024)(128)(4,1)}), s8[4194304]{0:T(1024)(128)(4,1)S(1)}, s32[]{:S(2)}) async-start(s8[16777216]{0:T(1024)(128)(4,1)} %bitcast.19), calls=%async_computation.10 | async-start | bytes 8388608
  2.7 37.3 %slice-start.7 = ((s8[16777216]{0:T(1024)(128)(4,1)}), s8[4194304]{0:T(1024)(128)(4,1)S(1)}, s32[]{:S(2)}) async-start(s8[16777216]{0:T(1024)(128)(4,1)} %bitcast.19), calls=%async_computation.11 | async-start | bytes 8388608
  2.7 37.3 %slice-start.8 = ((s8[16777216]{0:T(1024)(128)(4,1)}), s8[4194304]{0:T(1024)(128)(4,1)S(1)}, s32[]{:S(2)}) async-start(s8[16777216]{0:T(1024)(128)(4,1)} %bitcast.19), calls=%async_computation.12 | async-start | bytes 8388608
  2.8 26.9 %copy-start = (bf16[1,256,256]{2,1,0:T(8,128)(2,1)S(1)}, bf16[1,256,256]{2,1,0:T(8,128)(2,1)}, u32[]{:S(2)}) copy-start(bf16[1,256,256]{2,1,0:T(8,128)(2,1)} %param.11) | copy-start | bytes 393220
  2.8 26.9 %copy-start.1 = (bf16[1,256,256]{2,1,0:T(8,128)(2,1)S(1)}, bf16[1,256,256]{2,1,0:T(8,128)(2,1)}, u32[]{:S(2)}) copy-start(bf16[1,256,256]{2,1,0:T(8,128)(2,1)} %param.12) | copy-start | bytes 393220
  2.9 48.9 %copy-start.3 = (bf16[1,8192]{1,0:T(2,128)(2,1)S(1)}, bf16[1,8192]{1,0:T(2,128)(2,1)}, u32[]{:S(2)}) copy-start(bf16[1,8192]{1,0:T(2,128)(2,1)} %x_ref.1) | copy-start | bytes 49156

commit v4 on v3

--- a/solution.py
+++ b/solution.py
@@ -1,4 +1,4 @@
-import functools
+import math
 
 import jax
 import jax.numpy as jnp
@@ -26,13 +26,17 @@
     return pl.CostEstimate(flops=flops, bytes_accessed=size, transcendentals=0)
 
 
-def rope_tables(lengths):
+def table_kernel(len_ref, after_ref, t_ref):
     half = HD // 2
-    frequency = rope_theta ** (-jnp.arange(half, dtype=jnp.float32) * 2.0 / HD)
-    angles = lengths.astype(jnp.float32) * frequency
-    cosine = jnp.cos(angles)
+    lane = lax.broadcasted_iota(jnp.int32, (1, HD), 1)
+    place = jnp.where(lane < half, lane, lane - half).astype(jnp.float32)
+    frequency = jnp.exp(place * (-2.0 / HD * math.log(rope_theta)))
+    length = len_ref[0].astype(jnp.float32)
+    angles = length * frequency
     sine = jnp.sin(angles)
-    return jnp.stack([jnp.concatenate([cosine, cosine]), jnp.concatenate([-sine, sine])])
+    t_ref[0:1, :] = jnp.cos(angles)
+    t_ref[1:2, :] = jnp.where(lane < half, -sine, sine)
+    t_ref[2:3, :] = jnp.full((1, HD), length)
 
 
 def square_kernel(x_ref, f_ref, s_ref):
@@ -82,11 +86,12 @@
     return values * table[0:1, :] + swapped * table[1:2, :]
 
 
-def attend_kernel(joined_ref, length, table, k_ref, v_ref, o_ref):
+def attend_kernel(joined_ref, table, k_ref, v_ref, o_ref):
     groups, slots, head_dim = joined_ref.shape
     share = slots - 2
     capacity = k_ref.shape[0]
-    live = lax.broadcasted_iota(jnp.int32, (share, capacity), 1) < length
+    places = lax.broadcasted_iota(jnp.int32, (share, capacity), 1).astype(jnp.float32)
+    live = places < table[2:3, 0:1]
     for g in range(groups):
         lanes = slice(g * head_dim, (g + 1) * head_dim)
         query = (turn(joined_ref[g, :share, :], table) * head_dim ** (-0.5)).astype(jnp.bfloat16)
@@ -101,18 +106,19 @@
         expo = jnp.exp(scores - top)
         own_expo = jnp.exp(own - top)
         total = jnp.sum(expo, -1, keepdims=True) + own_expo
-        probs = (expo / total).astype(jnp.bfloat16)
+        share_of = 1.0 / total
+        probs = (expo * share_of).astype(jnp.bfloat16)
         mixed = jnp.dot(probs, v_ref[:, lanes], preferred_element_type=jnp.float32)
-        mixed = (mixed + (own_expo / total) * new_value).astype(jnp.bfloat16)
+        mixed = (mixed + (own_expo * share_of) * new_value).astype(jnp.bfloat16)
         for j in range(o_ref.shape[0]):
             o_ref[j, g * share : (g + 1) * share, :] = mixed
 
 
-def direct_kernel(core_ref, len_ref, parts_ref, table_ref, k_ref, v_ref, o_ref, joined):
+def direct_kernel(parts_ref, table_ref, k_ref, v_ref, o_ref, joined):
     half = parts_ref.shape[0] // 4
     cols = parts_ref.shape[2]
     groups, slots, _ = joined.shape
-    first = core_ref[0] * half
+    first = lax.axis_index("narrow") * half
     for b in range(half):
         for c in range(cols // LANES):
             piece = b * (cols // LANES) + c
@@ -120,17 +126,17 @@
             joined[piece // slots, piece % slots : piece % slots + 1, :] = (
                 parts_ref[2 * (first + b), :, lanes] + parts_ref[2 * (first + b) + 1, :, lanes]
             )
-    attend_kernel(joined, len_ref[0], table_ref[...], k_ref, v_ref, o_ref)
-
-
-def given_kernel(len_ref, joined_ref, table_ref, k_ref, v_ref, o_ref):
-    attend_kernel(joined_ref, len_ref[0], table_ref[...], k_ref, v_ref, o_ref)
-
-
-def add_kernel(core_ref, x_ref, parts_ref, o_ref):
+    attend_kernel(joined, table_ref[...], k_ref, v_ref, o_ref)
+
+
+def given_kernel(joined_ref, table_ref, k_ref, v_ref, o_ref):
+    attend_kernel(joined_ref, table_ref[...], k_ref, v_ref, o_ref)
+
+
+def add_kernel(x_ref, parts_ref, o_ref):
     half = parts_ref.shape[0] // 4
     lines, cols = parts_ref.shape[1:]
-    first = core_ref[0] * half
+    first = lax.axis_index("narrow") * half
     for b in range(half):
         one = parts_ref[2 * (first + b)].astype(jnp.float32)
         added = one + parts_ref[2 * (first + b) + 1].astype(jnp.float32)
@@ -149,8 +155,6 @@
 
 def body(hidden_in, norm_gain, qkv_weight, out_weight, cache_keys, cache_values, cache_lengths):
     wide = lax.axis_size("wide")
-    core = lax.axis_index("narrow").astype(jnp.int32).reshape(1)
-    hidden_in, core = lax.optimization_barrier((hidden_in, core))
     feats = hidden_in.shape[1]
     tiles = feats // LANES
     values, squares = pl.pallas_call(
@@ -162,10 +166,16 @@
         in_specs=[VMEM],
         out_specs=(VMEM, VMEM),
         compiler_params=params(4 << 20),
-        cost_estimate=cost(40_000_000_000, 64_000),
+        cost_estimate=cost(2_000_000_000, 64_000),
     )(hidden_in)
-    squares, lengths = lax.optimization_barrier((squares, cache_lengths))
-    table = rope_tables(lengths)
+    table = pl.pallas_call(
+        table_kernel,
+        out_shape=jax.ShapeDtypeStruct((3, HD), jnp.float32),
+        in_specs=[SMEM, VMEM],
+        out_specs=VMEM,
+        compiler_params=params(4 << 20),
+        cost_estimate=cost(1000, 1000),
+    )(cache_lengths, squares)
     others, table = lax.optimization_barrier((swap(squares), table))
     normed = pl.pallas_call(
         norm_kernel,
@@ -191,24 +201,24 @@
         mixed = pl.pallas_call(
             direct_kernel,
             out_shape=mixed_shape,
-            in_specs=[SMEM, SMEM, VMEM, VMEM, VMEM, VMEM],
+            in_specs=[VMEM, VMEM, VMEM, VMEM],
             out_specs=VMEM,
             scratch_shapes=[pltpu.VMEM((groups, slots, HD), jnp.float32)],
             compiler_params=params(4 << 20),
             cost_estimate=cost(1000, 40_000_000),
-        )(core, lengths, moved, table, keys, cached)
+        )(moved, table, keys, cached)
     else:
-        first = core[0] * (wide // 2)
+        first = lax.axis_index("narrow") * (wide // 2)
         joined = jnp.sum(moved.reshape(wide, 2, block), axis=1)
         joined = lax.dynamic_slice_in_dim(joined, first, wide // 2, 0)
         mixed = pl.pallas_call(
             given_kernel,
             out_shape=mixed_shape,
-            in_specs=[SMEM, VMEM, VMEM, VMEM, VMEM],
+            in_specs=[VMEM, VMEM, VMEM, VMEM],
             out_specs=VMEM,
             compiler_params=params(4 << 20),
             cost_estimate=cost(1000, 40_000_000),
-        )(lengths, joined.reshape(groups, slots, HD), table, keys, cached)
+        )(joined.reshape(groups, slots, HD), table, keys, cached)
     spread = exchange(mixed)
     lines = 2 if out_weight.shape[1] % (2 * LANES) == 0 else 1
     partial_out = product(spread.reshape(wide, depth), out_weight, 2, lines, jnp.bfloat16)
@@ -216,11 +226,11 @@
     return pl.pallas_call(
         add_kernel,
         out_shape=jax.ShapeDtypeStruct((1, feats), jnp.float32),
-        in_specs=[SMEM, VMEM, VMEM],
+        in_specs=[VMEM, VMEM],
         out_specs=VMEM,
         compiler_params=params(4 << 20),
         cost_estimate=cost(1000, 1_000_000),
-    )(core, hidden_in, parts)
+    )(hidden_in, parts)
 
 
 def solution(mesh):

time: 52.6 us -> 53.3 us (1.013)
  local copies, waits for them, and re-layouts: 0.94 us -> 1.84 us
    unnamed x30, local copies, waits for them, and re-layouts: 0.94 us -> 1.84 us
  transfers between devices with their start and end apart: 1 -> 1, of which waited for: 0 -> 0; matrix products, arithmetic and copies ran while one was open for 1% -> 0% of each run, Pallas kernels for 0% -> 0%
where the time goes in v4:
time: 53.3 us; the launch traced here: 53 us
  blocking collectives  43 us (81%)
  Pallas kernels  6.51 us (12%)
  local copies, waits for them, and re-layouts  1.84 us (3%)
  between operations  1.14 us (2%)
  starting transfers between devices  0.56 us (1%)
    all_to_all x4, blocking collectives, exchange(): return lax.all_to_all(x, axes, split_axis=0, concat_axis=0, tiled=True)  43 us
    pallas_call x2, Pallas kernels, product(): pl.pallas_call(product_kernel, out_shape=jax.ShapeDtypeStruct((rows * cop...  4.84 us
    unnamed x30, local copies, waits for them, and re-layouts  1.84 us
  transfers between devices with their start and end apart: 1, of which 0 were waited for; matrix products, arithmetic and copies ran while one was open for 0% of the time, Pallas kernels for 0%

profile of v4, /device:TPU:0, one launch (start us, length us, event | category | flops | bytes accessed | tf_op | source)
XLA Modules:
  0.0 53.0 jit_solution(8133337829129549444)
XLA Ops:
  0.0 0.0 copy-start.2
  0.0 0.8 %copy-done.2 = bf16[1,8192]{1,0:T(2,128)(2,1)S(1)} copy-done((bf16[1,8192]{1,0:T(2,128)(2,1)S(1)}, bf16[1,8192]{1,0:T(2,128)(2,1)}, u32[]{:S(2)}) %copy-start.2) | copy-done | bytes 16408
  0.8 0.0 slice-start
  0.8 0.6 %collective-permute-start = (f32[8,128]{1,0:T(8,128)S(1)}, f32[8,128]{1,0:T(8,128)S(1)}, u32[]{:S(2)}, u32[]{:S(2)}) collective-permute-start(f32[8,128]{1,0:T(8,128)S(1)} %get-tuple-element.10.after_ref.own_ref), channel_id=1, source_target_pairs={{0,1},{1,0},{2,3},{3,2},{4,5},{5,4},{6,7},{7,6},{8,9},{9,8},{10,11... | collective-permute-start | bytes 12296 | tf_op jit(solution)/shard_map/ppermute | solution.py:149
  2.3 0.1 shard_map.74.table_ref
  2.3 0.0 collective-permute-done.other_ref
  2.4 0.0 slice-start.5
  2.4 0.0 copy-start.4
  2.4 0.9 %copy-done.4 = f32[8192]{0:T(1024)S(1)} copy-done((f32[8192]{0:T(1024)S(1)}, f32[8192]{0:T(1024)}, u32[]{:S(2)}) %copy-start.4) | copy-done | bytes 32792
  3.3 0.0 slice-start.1
  3.3 0.0 slice-start.2
  3.3 0.0 slice-start.3
  3.3 0.0 slice-start.4
  3.3 0.0 slice-start.6
  3.3 0.0 slice-start.7
  3.3 0.0 slice-start.8
  3.3 0.1 shard_map.75
  3.5 0.0 copy-start
  3.5 0.0 copy-start.1
  3.5 0.0 copy-start.3
  3.5 14.6 %all_to_all.20 = bf16[8,64,128]{2,1,0:T(8,128)(2,1)S(1)} all-to-all(bf16[8,64,128]{2,1,0:T(8,128)(2,1)S(1)} %shard_map.75), channel_id=1, replica_groups=mesh['group'=2,'wide'=8,'narrow'=2] {'wide'}, dimensions={0} | all-to-all | bytes 262144 | tf_op jit(solution)/shard_map/all_to_all | solution.py:153
  18.1 0.1 copy.12
  18.2 0.0 slice-done
  18.2 0.0 slice-done.1
  18.2 0.0 slice-done.2
  18.2 0.0 slice-done.3
  18.2 0.0 slice-done.4
  18.3 2.5 %shard_map.76 = f32[16,1,1152]{2,1,0:T(1,128)S(1)} custom-call(bf16[8,8192]{1,0:T(8,128)(2,1)S(1)} %bitcast.15, bf16[8192,1152]{1,0:T(8,128)(2,1)S(1)} %bitcast.12), custom_call_target="tpu_custom_call" | custom-call | flops 150994944 | bytes 18874368 | tf_op jit(solution)/shard_map/pallas_call | solution.py:73
  20.8 9.6 %all_to_all.21.parts_ref = f32[16,1,1152]{2,1,0:T(1,128)S(1)} all-to-all(f32[16,1,1152]{2,1,0:T(1,128)S(1)} %shard_map.76), channel_id=1, replica_groups=mesh['group'=2,'wide'=8,'narrow'=2] {'wide','narrow'}, dimensions={0} | all-to-all | bytes 147456 | tf_op jit(solution)/shard_map/all_to_all | solution.py:153
  30.4 0.0 copy-done
  30.4 0.0 copy-done.1
  30.4 0.8 %shard_map.77 = bf16[8,32,128]{2,1,0:T(8,128)(2,1)S(1)} custom-call(f32[16,1,1152]{2,1,0:T(1,128)S(1)} %all_to_all.21.parts_ref, f32[3,128]{1,0:T(4,128)S(1)} %shard_map.74.table_ref, bf16[256,256]{1,0:T(8,128)(2,1)S(1)} %bitcast.17, bf16[256,256]{1,0:T(8,128)(2,1)S(1)} %bitcast.18), custom_call_target="tpu_custom_call" | custom-call | flops 1000 | bytes 40000000 | tf_op jit(solution)/shard_map/pallas_call | solution.py:201
  31.2 9.3 %all_to_all.22 = bf16[8,32,128]{2,1,0:T(8,128)(2,1)S(1)} all-to-all(bf16[8,32,128]{2,1,0:T(8,128)(2,1)S(1)} %shard_map.77), channel_id=1, replica_groups=mesh['group'=2,'wide'=8,'narrow'=2] {'wide'}, dimensions={0} | all-to-all | bytes 131072 | tf_op jit(solution)/shard_map/all_to_all | solution.py:153
  40.5 0.0 slice-done.5
  40.6 0.0 slice-done.6
  40.6 0.0 slice-done.7
  40.6 0.0 slice-done.8
  40.6 2.3 %shard_map.78 = bf16[16,2,1024]{2,1,0:T(2,128)(2,1)S(1)} custom-call(bf16[8,4096]{1,0:T(8,128)(2,1)S(1)} %bitcast.16, bf16[4096,2048]{1,0:T(8,128)(2,1)S(1)} %bitcast.14), custom_call_target="tpu_custom_call" | custom-call | flops 134217728 | bytes 16777216 | tf_op jit(solution)/shard_map/pallas_call | solution.py:73
  42.9 9.5 %all_to_all.23.parts_ref = bf16[16,2,1024]{2,1,0:T(2,128)(2,1)S(1)} all-to-all(bf16[16,2,1024]{2,1,0:T(2,128)(2,1)S(1)} %shard_map.78), channel_id=1, replica_groups=mesh['group'=2,'wide'=8,'narrow'=2] {'wide','narrow'}, dimensions={0} | all-to-all | bytes 131072 | tf_op jit(solution)/shard_map/all_to_all | solution.py:153
  52.4 0.0 copy-done.3
  52.4 0.6 %shard_map.79 = f32[1,8192]{1,0:T(1,128)} custom-call(bf16[1,8192]{1,0:T(2,128)(2,1)S(1)} %copy-done.3, bf16[16,2,1024]{2,1,0:T(2,128)(2,1)S(1)} %all_to_all.23.parts_ref), custom_call_target="tpu_custom_call" | custom-call | flops 1000 | bytes 1000000 | tf_op jit(solution)/shard_map/pallas_call | solution.py:226
  (4 shorter events, 0.1 us)
Async XLA Ops:
  0.0 0.8 %copy-start.2 = (bf16[1,8192]{1,0:T(2,128)(2,1)S(1)}, bf16[1,8192]{1,0:T(2,128)(2,1)}, u32[]{:S(2)}) copy-start(bf16[1,8192]{1,0:T(2,128)(2,1)} %x_ref.3) | copy-start | bytes 49156
  0.8 17.4 %slice-start = ((s8[18874368]{0:T(1024)(128)(4,1)}), s8[4194304]{0:T(1024)(128)(4,1)S(1)}, s32[]{:S(2)}) async-start(s8[18874368]{0:T(1024)(128)(4,1)} %bitcast.11), calls=%async_computation.4 | async-start | bytes 8388608
  0.8 1.6 %collective-permute-start = (f32[8,128]{1,0:T(8,128)S(1)}, f32[8,128]{1,0:T(8,128)S(1)}, u32[]{:S(2)}, u32[]{:S(2)}) collective-permute-start(f32[8,128]{1,0:T(8,128)S(1)} %get-tuple-element.10.after_ref.own_ref), channel_id=1, source_target_pairs={{0,1},{1,0},{2,3},{3,2},{4,5},{5,4},{6,7},{7,6},{8,9},{9,8},{10,11... | collective-permute-start | bytes 12296 | tf_op jit(solution)/shard_map/ppermute | solution.py:149
  2.4 38.2 %slice-start.5 = ((s8[16777216]{0:T(1024)(128)(4,1)}), s8[4194304]{0:T(1024)(128)(4,1)S(1)}, s32[]{:S(2)}) async-start(s8[16777216]{0:T(1024)(128)(4,1)} %bitcast.13), calls=%async_computation.9 | async-start | bytes 8388608
  2.4 0.9 %copy-start.4 = (f32[8192]{0:T(1024)S(1)}, f32[8192]{0:T(1024)}, u32[]{:S(2)}) copy-start(f32[8192]{0:T(1024)} %param.8) | copy-start | bytes 98308
  3.3 14.9 %slice-start.1 = ((s8[18874368]{0:T(1024)(128)(4,1)}), s8[4194304]{0:T(1024)(128)(4,1)S(1)}, s32[]{:S(2)}) async-start(s8[18874368]{0:T(1024)(128)(4,1)} %bitcast.11), calls=%async_computation.5 | async-start | bytes 8388608
  3.3 14.9 %slice-start.2 = ((s8[18874368]{0:T(1024)(128)(4,1)}), s8[4194304]{0:T(1024)(128)(4,1)S(1)}, s32[]{:S(2)}) async-start(s8[18874368]{0:T(1024)(128)(4,1)} %bitcast.11), calls=%async_computation.6 | async-start | bytes 8388608
  3.3 14.9 %slice-start.3 = ((s8[18874368]{0:T(1024)(128)(4,1)}), s8[4194304]{0:T(1024)(128)(4,1)S(1)}, s32[]{:S(2)}) async-start(s8[18874368]{0:T(1024)(128)(4,1)} %bitcast.11), calls=%async_computation.7 | async-start | bytes 8388608
  3.3 15.0 %slice-start.4 = ((s8[18874368]{0:T(1024)(128)(4,1)}), s8[2097152]{0:T(1024)(128)(4,1)S(1)}, s32[]{:S(2)}) async-start(s8[18874368]{0:T(1024)(128)(4,1)} %bitcast.11), calls=%async_computation.8 | async-start | bytes 4194304
  3.3 37.3 %slice-start.6 = ((s8[16777216]{0:T(1024)(128)(4,1)}), s8[4194304]{0:T(1024)(128)(4,1)S(1)}, s32[]{:S(2)}) async-start(s8[16777216]{0:T(1024)(128)(4,1)} %bitcast.13), calls=%async_computation.10 | async-start | bytes 8388608
  3.3 37.3 %slice-start.7 = ((s8[16777216]{0:T(1024)(128)(4,1)}), s8[4194304]{0:T(1024)(128)(4,1)S(1)}, s32[]{:S(2)}) async-start(s8[16777216]{0:T(1024)(128)(4,1)} %bitcast.13), calls=%async_computation.11 | async-start | bytes 8388608
  3.3 37.3 %slice-start.8 = ((s8[16777216]{0:T(1024)(128)(4,1)}), s8[4194304]{0:T(1024)(128)(4,1)S(1)}, s32[]{:S(2)}) async-start(s8[16777216]{0:T(1024)(128)(4,1)} %bitcast.13), calls=%async_computation.12 | async-start | bytes 8388608
  3.5 26.9 %copy-start = (bf16[1,256,256]{2,1,0:T(8,128)(2,1)S(1)}, bf16[1,256,256]{2,1,0:T(8,128)(2,1)}, u32[]{:S(2)}) copy-start(bf16[1,256,256]{2,1,0:T(8,128)(2,1)} %param.11) | copy-start | bytes 393220
  3.5 26.9 %copy-start.1 = (bf16[1,256,256]{2,1,0:T(8,128)(2,1)S(1)}, bf16[1,256,256]{2,1,0:T(8,128)(2,1)}, u32[]{:S(2)}) copy-start(bf16[1,256,256]{2,1,0:T(8,128)(2,1)} %param.12) | copy-start | bytes 393220
  3.5 48.9 %copy-start.3 = (bf16[1,8192]{1,0:T(2,128)(2,1)S(1)}, bf16[1,8192]{1,0:T(2,128)(2,1)}, u32[]{:S(2)}) copy-start(bf16[1,8192]{1,0:T(2,128)(2,1)} %x_ref.3) | copy-start | bytes 49156

commit v5 on v4

--- a/solution.py
+++ b/solution.py
@@ -166,7 +166,7 @@
         in_specs=[VMEM],
         out_specs=(VMEM, VMEM),
         compiler_params=params(4 << 20),
-        cost_estimate=cost(2_000_000_000, 64_000),
+        cost_estimate=cost(8_000_000_000, 64_000),
     )(hidden_in)
     table = pl.pallas_call(
         table_kernel,
@@ -183,7 +183,7 @@
         in_specs=[VMEM] * 4,
         out_specs=VMEM,
         compiler_params=params(4 << 20),
-        cost_estimate=cost(40_000_000_000, 40_000_000),
+        cost_estimate=cost(200_000_000_000, 40_000_000),
     )(values, norm_gain.reshape(tiles, LANES), squares, others)
     gathered = exchange(normed)
     partial_qkv = product(gathered.reshape(wide, feats), qkv_weight, 2, 1, jnp.float32)

time: 53.3 us -> 52 us (0.976)
  local copies, waits for them, and re-layouts: 1.84 us -> 0.91 us
    unnamed x30 -> x16, local copies, waits for them, and re-layouts: 1.84 us -> 0.91 us
  transfers between devices with their start and end apart: 1 -> 1, of which waited for: 0 -> 1; matrix products, arithmetic and copies ran while one was open for 0% -> 0% of each run, Pallas kernels for 0% -> 0%
where the time goes in v5:
time: 52 us; the launch traced here: 51.7 us
  blocking collectives  42.9 us (82%)
  Pallas kernels  6.51 us (13%)
  local copies, waits for them, and re-layouts  0.91 us (2%)
  between operations  0.74 us (1%)
  starting transfers between devices  0.56 us (1%)
    all_to_all x4, blocking collectives, exchange(): return lax.all_to_all(x, axes, split_axis=0, concat_axis=0, tiled=True)  42.9 us
    pallas_call x2, Pallas kernels, product(): pl.pallas_call(product_kernel, out_shape=jax.ShapeDtypeStruct((rows * cop...  4.84 us
  transfers between devices with their start and end apart: 1, of which 1 were waited for; matrix products, arithmetic and copies ran while one was open for 0% of the time, Pallas kernels for 0%

profile of v5, /device:TPU:0, one launch (start us, length us, event | category | flops | bytes accessed | tf_op | source)
XLA Modules:
  0.0 51.7 jit_solution(7874837770718376042)
XLA Ops:
  0.0 0.0 copy-start.4
  0.0 0.8 %copy-done.4 = bf16[1,8192]{1,0:T(2,128)(2,1)S(1)} copy-done((bf16[1,8192]{1,0:T(2,128)(2,1)S(1)}, bf16[1,8192]{1,0:T(2,128)(2,1)}, u32[]{:S(2)}) %copy-start.4) | copy-done | bytes 16408
  0.8 0.0 copy-start.6
  0.8 0.6 %collective-permute-start = (f32[8,128]{1,0:T(8,128)S(1)}, f32[8,128]{1,0:T(8,128)S(1)}, u32[]{:S(2)}, u32[]{:S(2)}) collective-permute-start(f32[8,128]{1,0:T(8,128)S(1)} %get-tuple-element.10.after_ref.own_ref), channel_id=1, source_target_pairs={{0,1},{1,0},{2,3},{3,2},{4,5},{5,4},{6,7},{7,6},{8,9},{9,8},{10,11... | collective-permute-start | bytes 12296 | tf_op jit(solution)/shard_map/ppermute | solution.py:149
  2.0 0.1 shard_map.74.table_ref
  2.1 0.1 collective-permute-done.other_ref
  2.2 0.0 copy-done.6
  2.2 0.0 copy-start
  2.2 0.1 shard_map.75
  2.3 0.0 copy-start.2
  2.3 0.0 copy-start.3
  2.3 0.0 copy-start.1
  2.4 0.0 copy-start.5
  2.4 14.5 %all_to_all.20 = bf16[8,64,128]{2,1,0:T(8,128)(2,1)S(1)} all-to-all(bf16[8,64,128]{2,1,0:T(8,128)(2,1)S(1)} %shard_map.75), channel_id=1, replica_groups=mesh['group'=2,'wide'=8,'narrow'=2] {'wide'}, dimensions={0} | all-to-all | bytes 262144 | tf_op jit(solution)/shard_map/all_to_all | solution.py:153
  16.9 0.1 copy.12
  17.0 0.0 copy-done
  17.0 2.5 %shard_map.76 = f32[16,1,1152]{2,1,0:T(1,128)S(1)} custom-call(bf16[8,8192]{1,0:T(8,128)(2,1)S(1)} %bitcast.11, bf16[8192,1152]{1,0:T(8,128)(2,1)S(1)} %copy-done), custom_call_target="tpu_custom_call" | custom-call | flops 150994944 | bytes 18874368 | tf_op jit(solution)/shard_map/pallas_call | solution.py:73
  19.6 9.6 %all_to_all.21.parts_ref = f32[16,1,1152]{2,1,0:T(1,128)S(1)} all-to-all(f32[16,1,1152]{2,1,0:T(1,128)S(1)} %shard_map.76), channel_id=1, replica_groups=mesh['group'=2,'wide'=8,'narrow'=2] {'wide','narrow'}, dimensions={0} | all-to-all | bytes 147456 | tf_op jit(solution)/shard_map/all_to_all | solution.py:153
  29.1 0.0 copy-done.2
  29.1 0.0 copy-done.3
  29.1 0.8 %shard_map.77 = bf16[8,32,128]{2,1,0:T(8,128)(2,1)S(1)} custom-call(f32[16,1,1152]{2,1,0:T(1,128)S(1)} %all_to_all.21.parts_ref, f32[3,128]{1,0:T(4,128)S(1)} %shard_map.74.table_ref, bf16[256,256]{1,0:T(8,128)(2,1)S(1)} %bitcast.13, bf16[256,256]{1,0:T(8,128)(2,1)S(1)} %bitcast.14), custom_call_target="tpu_custom_call" | custom-call | flops 1000 | bytes 40000000 | tf_op jit(solution)/shard_map/pallas_call | solution.py:201
  30.0 9.3 %all_to_all.22 = bf16[8,32,128]{2,1,0:T(8,128)(2,1)S(1)} all-to-all(bf16[8,32,128]{2,1,0:T(8,128)(2,1)S(1)} %shard_map.77), channel_id=1, replica_groups=mesh['group'=2,'wide'=8,'narrow'=2] {'wide'}, dimensions={0} | all-to-all | bytes 131072 | tf_op jit(solution)/shard_map/all_to_all | solution.py:153
  39.3 0.0 copy-done.1
  39.3 2.3 %shard_map.78 = bf16[16,2,1024]{2,1,0:T(2,128)(2,1)S(1)} custom-call(bf16[8,4096]{1,0:T(8,128)(2,1)S(1)} %bitcast.12, bf16[4096,2048]{1,0:T(8,128)(2,1)S(1)} %copy-done.1), custom_call_target="tpu_custom_call" | custom-call | flops 134217728 | bytes 16777216 | tf_op jit(solution)/shard_map/pallas_call | solution.py:73
  41.6 9.5 %all_to_all.23.parts_ref = bf16[16,2,1024]{2,1,0:T(2,128)(2,1)S(1)} all-to-all(bf16[16,2,1024]{2,1,0:T(2,128)(2,1)S(1)} %shard_map.78), channel_id=1, replica_groups=mesh['group'=2,'wide'=8,'narrow'=2] {'wide','narrow'}, dimensions={0} | all-to-all | bytes 131072 | tf_op jit(solution)/shard_map/all_to_all | solution.py:153
  51.1 0.0 copy-done.5
  51.1 0.6 %shard_map.79 = f32[1,8192]{1,0:T(1,128)} custom-call(bf16[1,8192]{1,0:T(2,128)(2,1)S(1)} %copy-done.5, bf16[16,2,1024]{2,1,0:T(2,128)(2,1)S(1)} %all_to_all.23.parts_ref), custom_call_target="tpu_custom_call" | custom-call | flops 1000 | bytes 1000000 | tf_op jit(solution)/shard_map/pallas_call | solution.py:226
  (2 shorter events, 0.1 us)
Async XLA Ops:
  0.0 0.8 %copy-start.4 = (bf16[1,8192]{1,0:T(2,128)(2,1)S(1)}, bf16[1,8192]{1,0:T(2,128)(2,1)}, u32[]{:S(2)}) copy-start(bf16[1,8192]{1,0:T(2,128)(2,1)} %x_ref.3) | copy-start | bytes 49156
  0.8 1.4 %copy-start.6 = (f32[8192]{0:T(1024)S(1)}, f32[8192]{0:T(1024)}, u32[]{:S(2)}) copy-start(f32[8192]{0:T(1024)} %param.8) | copy-start | bytes 98308
  0.8 1.4 %collective-permute-start = (f32[8,128]{1,0:T(8,128)S(1)}, f32[8,128]{1,0:T(8,128)S(1)}, u32[]{:S(2)}, u32[]{:S(2)}) collective-permute-start(f32[8,128]{1,0:T(8,128)S(1)} %get-tuple-element.10.after_ref.own_ref), channel_id=1, source_target_pairs={{0,1},{1,0},{2,3},{3,2},{4,5},{5,4},{6,7},{7,6},{8,9},{9,8},{10,11... | collective-permute-start | bytes 12296 | tf_op jit(solution)/shard_map/ppermute | solution.py:149
  2.2 14.8 %copy-start = (bf16[8192,1152]{1,0:T(8,128)(2,1)S(1)}, bf16[8192,1152]{1,0:T(8,128)(2,1)}, u32[]{:S(2)}) copy-start(bf16[8192,1152]{1,0:T(8,128)(2,1)} %w_ref.2) | copy-start | bytes 56623108
  2.3 26.8 %copy-start.2 = (bf16[1,256,256]{2,1,0:T(8,128)(2,1)S(1)}, bf16[1,256,256]{2,1,0:T(8,128)(2,1)}, u32[]{:S(2)}) copy-start(bf16[1,256,256]{2,1,0:T(8,128)(2,1)} %param.11) | copy-start | bytes 393220
  2.3 26.8 %copy-start.3 = (bf16[1,256,256]{2,1,0:T(8,128)(2,1)S(1)}, bf16[1,256,256]{2,1,0:T(8,128)(2,1)}, u32[]{:S(2)}) copy-start(bf16[1,256,256]{2,1,0:T(8,128)(2,1)} %param.12) | copy-start | bytes 393220
  2.3 36.9 %copy-start.1 = (bf16[4096,2048]{1,0:T(8,128)(2,1)S(1)}, bf16[4096,2048]{1,0:T(8,128)(2,1)}, u32[]{:S(2)}) copy-start(bf16[4096,2048]{1,0:T(8,128)(2,1)} %w_ref.3) | copy-start | bytes 50331652
  2.4 48.7 %copy-start.5 = (bf16[1,8192]{1,0:T(2,128)(2,1)S(1)}, bf16[1,8192]{1,0:T(2,128)(2,1)}, u32[]{:S(2)}) copy-start(bf16[1,8192]{1,0:T(2,128)(2,1)} %x_ref.3) | copy-start | bytes 49156

commit v6 on v5

--- a/solution.py
+++ b/solution.py
@@ -205,7 +205,7 @@
             out_specs=VMEM,
             scratch_shapes=[pltpu.VMEM((groups, slots, HD), jnp.float32)],
             compiler_params=params(4 << 20),
-            cost_estimate=cost(1000, 40_000_000),
+            cost_estimate=cost(200_000_000_000, 40_000_000),
         )(moved, table, keys, cached)
     else:
         first = lax.axis_index("narrow") * (wide // 2)
@@ -217,7 +217,7 @@
             in_specs=[VMEM, VMEM, VMEM, VMEM],
             out_specs=VMEM,
             compiler_params=params(4 << 20),
-            cost_estimate=cost(1000, 40_000_000),
+            cost_estimate=cost(200_000_000_000, 40_000_000),
         )(joined.reshape(groups, slots, HD), table, keys, cached)
     spread = exchange(mixed)
     lines = 2 if out_weight.shape[1] % (2 * LANES) == 0 else 1

time: 52 us -> 52.5 us (level)
    all_to_all x4, blocking collectives: 42.9 us -> 43.4 us  [exchange(): return lax.all_to_all(x, axes, split_axis=0, concat_axis=0, tiled=True)]
where the time goes in v6:
time: 52.5 us; the launch traced here: 52.2 us
  blocking collectives  43.4 us (83%)
  Pallas kernels  6.51 us (12%)
  local copies, waits for them, and re-layouts  0.9 us (2%)
  between operations  0.73 us (1%)
  starting transfers between devices  0.56 us (1%)
    all_to_all x4, blocking collectives, exchange(): return lax.all_to_all(x, axes, split_axis=0, concat_axis=0, tiled=True)  43.4 us
    pallas_call x2, Pallas kernels, product(): pl.pallas_call(product_kernel, out_shape=jax.ShapeDtypeStruct((rows * cop...  4.84 us
  transfers between devices with their start and end apart: 1, of which 1 were waited for; matrix products, arithmetic and copies ran while one was open for 0% of the time, Pallas kernels for 0%

profile of v6, /device:TPU:0, one launch (start us, length us, event | category | flops | bytes accessed | tf_op | source)
XLA Modules:
  0.0 52.2 jit_solution(7997237183069279656)
XLA Ops:
  0.0 0.0 copy-start.2
  0.0 0.8 %copy-done.2 = bf16[1,8192]{1,0:T(2,128)(2,1)S(1)} copy-done((bf16[1,8192]{1,0:T(2,128)(2,1)S(1)}, bf16[1,8192]{1,0:T(2,128)(2,1)}, u32[]{:S(2)}) %copy-start.2) | copy-done | bytes 16408
  0.8 0.0 copy-start.6
  0.8 0.6 %collective-permute-start = (f32[8,128]{1,0:T(8,128)S(1)}, f32[8,128]{1,0:T(8,128)S(1)}, u32[]{:S(2)}, u32[]{:S(2)}) collective-permute-start(f32[8,128]{1,0:T(8,128)S(1)} %get-tuple-element.10.after_ref.own_ref), channel_id=1, source_target_pairs={{0,1},{1,0},{2,3},{3,2},{4,5},{5,4},{6,7},{7,6},{8,9},{9,8},{10,11... | collective-permute-start | bytes 12296 | tf_op jit(solution)/shard_map/ppermute | solution.py:149
  2.0 0.1 shard_map.74.table_ref
  2.1 0.1 collective-permute-done.other_ref
  2.2 0.0 copy-done.6
  2.2 0.0 copy-start
  2.2 0.1 shard_map.75
  2.3 0.0 copy-start.4
  2.3 0.0 copy-start.5
  2.3 14.5 %all_to_all.20 = bf16[8,64,128]{2,1,0:T(8,128)(2,1)S(1)} all-to-all(bf16[8,64,128]{2,1,0:T(8,128)(2,1)S(1)} %shard_map.75), channel_id=1, replica_groups=mesh['group'=2,'wide'=8,'narrow'=2] {'wide'}, dimensions={0} | all-to-all | bytes 262144 | tf_op jit(solution)/shard_map/all_to_all | solution.py:153
  16.9 0.1 copy.12
  17.0 0.0 copy-done
  17.0 2.5 %shard_map.76 = f32[16,1,1152]{2,1,0:T(1,128)S(1)} custom-call(bf16[8,8192]{1,0:T(8,128)(2,1)S(1)} %bitcast.11, bf16[8192,1152]{1,0:T(8,128)(2,1)S(1)} %copy-done), custom_call_target="tpu_custom_call" | custom-call | flops 150994944 | bytes 18874368 | tf_op jit(solution)/shard_map/pallas_call | solution.py:73
  19.5 9.6 %all_to_all.21.parts_ref = f32[16,1,1152]{2,1,0:T(1,128)S(1)} all-to-all(f32[16,1,1152]{2,1,0:T(1,128)S(1)} %shard_map.76), channel_id=1, replica_groups=mesh['group'=2,'wide'=8,'narrow'=2] {'wide','narrow'}, dimensions={0} | all-to-all | bytes 147456 | tf_op jit(solution)/shard_map/all_to_all | solution.py:153
  29.1 0.0 copy-done.4
  29.1 0.0 copy-done.5
  29.1 0.0 copy-start.1
  29.1 0.0 copy-start.3
  29.1 0.8 %shard_map.77 = bf16[8,32,128]{2,1,0:T(8,128)(2,1)S(1)} custom-call(f32[16,1,1152]{2,1,0:T(1,128)S(1)} %all_to_all.21.parts_ref, f32[3,128]{1,0:T(4,128)S(1)} %shard_map.74.table_ref, bf16[256,256]{1,0:T(8,128)(2,1)S(1)} %bitcast.13, bf16[256,256]{1,0:T(8,128)(2,1)S(1)} %bitcast.14), custom_call_target="tpu_custom_call" | custom-call | flops 199999995904 | bytes 40000000 | tf_op jit(solution)/shard_map/pallas_call | solution.py:201
  29.9 9.8 %all_to_all.22 = bf16[8,32,128]{2,1,0:T(8,128)(2,1)S(1)} all-to-all(bf16[8,32,128]{2,1,0:T(8,128)(2,1)S(1)} %shard_map.77), channel_id=1, replica_groups=mesh['group'=2,'wide'=8,'narrow'=2] {'wide'}, dimensions={0} | all-to-all | bytes 131072 | tf_op jit(solution)/shard_map/all_to_all | solution.py:153
  39.8 0.0 copy-done.1
  39.8 2.3 %shard_map.78 = bf16[16,2,1024]{2,1,0:T(2,128)(2,1)S(1)} custom-call(bf16[8,4096]{1,0:T(8,128)(2,1)S(1)} %bitcast.12, bf16[4096,2048]{1,0:T(8,128)(2,1)S(1)} %copy-done.1), custom_call_target="tpu_custom_call" | custom-call | flops 134217728 | bytes 16777216 | tf_op jit(solution)/shard_map/pallas_call | solution.py:73
  42.1 9.5 %all_to_all.23.parts_ref = bf16[16,2,1024]{2,1,0:T(2,128)(2,1)S(1)} all-to-all(bf16[16,2,1024]{2,1,0:T(2,128)(2,1)S(1)} %shard_map.78), channel_id=1, replica_groups=mesh['group'=2,'wide'=8,'narrow'=2] {'wide','narrow'}, dimensions={0} | all-to-all | bytes 131072 | tf_op jit(solution)/shard_map/all_to_all | solution.py:153
  51.6 0.0 copy-done.3
  51.6 0.6 %shard_map.79 = f32[1,8192]{1,0:T(1,128)} custom-call(bf16[1,8192]{1,0:T(2,128)(2,1)S(1)} %copy-done.3, bf16[16,2,1024]{2,1,0:T(2,128)(2,1)S(1)} %all_to_all.23.parts_ref), custom_call_target="tpu_custom_call" | custom-call | flops 1000 | bytes 1000000 | tf_op jit(solution)/shard_map/pallas_call | solution.py:226
  (2 shorter events, 0.1 us)
Async XLA Ops:
  0.0 0.8 %copy-start.2 = (bf16[1,8192]{1,0:T(2,128)(2,1)S(1)}, bf16[1,8192]{1,0:T(2,128)(2,1)}, u32[]{:S(2)}) copy-start(bf16[1,8192]{1,0:T(2,128)(2,1)} %x_ref.3) | copy-start | bytes 49156
  0.8 1.4 %copy-start.6 = (f32[8192]{0:T(1024)S(1)}, f32[8192]{0:T(1024)}, u32[]{:S(2)}) copy-start(f32[8192]{0:T(1024)} %param.8) | copy-start | bytes 98308
  0.8 1.4 %collective-permute-start = (f32[8,128]{1,0:T(8,128)S(1)}, f32[8,128]{1,0:T(8,128)S(1)}, u32[]{:S(2)}, u32[]{:S(2)}) collective-permute-start(f32[8,128]{1,0:T(8,128)S(1)} %get-tuple-element.10.after_ref.own_ref), channel_id=1, source_target_pairs={{0,1},{1,0},{2,3},{3,2},{4,5},{5,4},{6,7},{7,6},{8,9},{9,8},{10,11... | collective-permute-start | bytes 12296 | tf_op jit(solution)/shard_map/ppermute | solution.py:149
  2.2 14.8 %copy-start = (bf16[8192,1152]{1,0:T(8,128)(2,1)S(1)}, bf16[8192,1152]{1,0:T(8,128)(2,1)}, u32[]{:S(2)}) copy-start(bf16[8192,1152]{1,0:T(8,128)(2,1)} %w_ref.2) | copy-start | bytes 56623108
  2.3 26.8 %copy-start.4 = (bf16[1,256,256]{2,1,0:T(8,128)(2,1)S(1)}, bf16[1,256,256]{2,1,0:T(8,128)(2,1)}, u32[]{:S(2)}) copy-start(bf16[1,256,256]{2,1,0:T(8,128)(2,1)} %param.11) | copy-start | bytes 393220
  2.3 26.8 %copy-start.5 = (bf16[1,256,256]{2,1,0:T(8,128)(2,1)S(1)}, bf16[1,256,256]{2,1,0:T(8,128)(2,1)}, u32[]{:S(2)}) copy-start(bf16[1,256,256]{2,1,0:T(8,128)(2,1)} %param.12) | copy-start | bytes 393220
  29.1 10.7 %copy-start.1 = (bf16[4096,2048]{1,0:T(8,128)(2,1)S(1)}, bf16[4096,2048]{1,0:T(8,128)(2,1)}, u32[]{:S(2)}) copy-start(bf16[4096,2048]{1,0:T(8,128)(2,1)} %w_ref.3) | copy-start | bytes 50331652
  29.1 22.5 %copy-start.3 = (bf16[1,8192]{1,0:T(2,128)(2,1)S(1)}, bf16[1,8192]{1,0:T(2,128)(2,1)}, u32[]{:S(2)}) copy-start(bf16[1,8192]{1,0:T(2,128)(2,1)} %x_ref.3) | copy-start | bytes 49156
